TPU v7x, 512 devices: a whole 4x8x8 slice. The times are simulated.
512 devices in a mesh: gx: 8 (over y), gy: 8 (over x, z_lo), gz: 8 (over z_hi, core).
Axes of the slice: x: 4, y: 8, z: 8 (z_hi: 4, z_lo: 2; z = z_hi * 2 + z_lo), core: 2. Of those that a mesh axis runs over, the one named last changes fastest.
Arguments:
- features: bfloat16 [64, 32, 32, 512], P('gx', 'gy', 'gz'), may hold values from -31 to 31, as said below
- grad_y: bfloat16 [64, 32, 32, 512], P('gx', 'gy', 'gz'), may hold values from -6 to 6
- attn_out: bfloat16 [64, 32, 32, 512], P('gx', 'gy', 'gz'), may hold values from -3 to 3
- w_query: bfloat16 [512, 512], P('gz'), may hold values from -0.25 to 0.25
- w_key: bfloat16 [512, 512], P('gz'), may hold values from -0.25 to 0.25
- w_value: bfloat16 [512, 512], P('gz'), may hold values from -0.25 to 0.25
- w_out: bfloat16 [512, 512], P('gz'), may hold values from -0.25 to 0.25
Outputs:
- grad_x: bfloat16 [64, 32, 32, 512], P('gx', 'gy', 'gz')
- grad_query: float32 [512, 512], P('gz')
- grad_key: float32 [512, 512], P('gz')
- grad_value: float32 [512, 512], P('gz')
- grad_out: float32 [512, 512], P('gz')
Inputs may be any that keep to these rules, and one draw needn't show every extreme that they name: features of the patch tokens.
All inputs are finite; a program needn't handle non-finite values.
Results may differ from a plain program's by a relative error of at most 0.018.
Values may be sent and summed in bfloat16 or wider, within the bound.
A program may use at most 64 MiB of HBM per device.

v0:
```python
import math

import jax
import jax.numpy as jnp
from jax import lax
from jax.sharding import PartitionSpec as P

HEADS = 8


def from_partner(block, axis, distance):
    count = lax.axis_size(axis)
    route = []
    for low in range(count):
        high = low | 1 << distance
        if high != low and high < count:
            route += [(low, high), (high, low)]
    return lax.ppermute(block, axis, route)


def shifted(value, axis, steps):
    count = lax.axis_size(axis)
    pairs = [(source, (source + steps) % count) for source in range(count)]
    return lax.ppermute(value, axis, pairs)


def channel_part(stacked, start, count):
    return lax.dynamic_slice_in_dim(stacked, start, count, stacked.ndim - 1)


def ordered_join(first_bit, own_part, other_part, axis):
    lower = jnp.where(first_bit == 0, own_part, other_part)
    upper = jnp.where(first_bit == 0, other_part, own_part)
    return jnp.concatenate([lower, upper], axis=axis)


def transpose_dot(left, right):
    return lax.dot_general(
        left, right, (((1,), (1,)), ((), ())), preferred_element_type=jnp.float32
    )


def token_dot(left, right):
    return lax.dot_general(
        left, right, (((0,), (0,)), ((), ())), preferred_element_type=jnp.float32
    )


def on_device(features, grad_y, attn_out, w_query, w_key, w_value, w_out):
    block_edge, half_y, half_z, width = features.shape
    local_tokens = block_edge * half_y * half_z
    block_tokens = block_edge**3
    half_width = width // 2
    quarter = width // 4
    head_dim = width // HEADS
    group_heads = HEADS // 4
    score_scale = 1.0 / math.sqrt(head_dim)
    z_bit = lax.axis_index("gz") % 2
    y_bit = lax.axis_index("gy") % 2
    full_query, full_key, full_value, full_out = (
        lax.all_gather(w_query, "gz", axis=0, tiled=True),
        lax.all_gather(w_key, "gz", axis=0, tiled=True),
        lax.all_gather(w_value, "gz", axis=0, tiled=True),
        lax.all_gather(w_out, "gz", axis=0, tiled=True),
    )
    feature_rows = features.reshape(local_tokens, width)
    dy_rows = grad_y.reshape(local_tokens, width)
    saved_rows = attn_out.reshape(local_tokens, width)
    out_term = token_dot(saved_rows, dy_rows)
    query = jnp.dot(feature_rows, full_query, preferred_element_type=jnp.float32).astype(
        jnp.bfloat16
    )
    key_rows = jnp.dot(feature_rows, full_key, preferred_element_type=jnp.float32).astype(
        jnp.bfloat16
    )
    value_rows = jnp.dot(feature_rows, full_value, preferred_element_type=jnp.float32).astype(
        jnp.bfloat16
    )
    out_grad = transpose_dot(dy_rows, full_out).astype(jnp.bfloat16)
    stacked = jnp.stack([query, key_rows, value_rows, out_grad, saved_rows]).reshape(
        5, block_edge, half_y, half_z, width
    )
    kept_part = channel_part(stacked, z_bit * half_width, half_width)
    sent_part = channel_part(stacked, (1 - z_bit) * half_width, half_width)
    came_part = from_partner(sent_part, "gz", 0)
    by_z = ordered_join(z_bit, kept_part, came_part, 3)
    kept_part = channel_part(by_z, y_bit * quarter, quarter)
    sent_part = channel_part(by_z, (1 - y_bit) * quarter, quarter)
    came_part = from_partner(sent_part, "gy", 0)
    whole_block = ordered_join(y_bit, kept_part, came_part, 2).reshape(5, block_tokens, quarter)
    query_heads = whole_block[0].reshape(block_tokens, group_heads, head_dim)
    grad_heads = whole_block[3].reshape(block_tokens, group_heads, head_dim)
    products = whole_block[3].astype(jnp.float32) * whole_block[4].astype(jnp.float32)
    row_delta = jnp.sum(products.reshape(block_tokens, group_heads, head_dim), axis=2).T
    own_pair = whole_block[1:3]
    key_list = [own_pair]
    for offset in (1, -1):
        key_list.append(shifted(own_pair, "gx", offset))
    for offset in (2, -2):
        key_list.append(shifted(own_pair, "gy", offset))
    for offset in (2, -2):
        key_list.append(shifted(own_pair, "gz", offset))
    nearby = jnp.stack(key_list)

    def first_pass(carry, key_value):
        row_top, row_total = carry
        key_heads = key_value[0].reshape(block_tokens, group_heads, head_dim)
        scores = (
            jnp.einsum("qhd,khd->hqk", query_heads, key_heads, preferred_element_type=jnp.float32)
            * score_scale
        )
        new_top = jnp.maximum(row_top, jnp.max(scores, axis=2))
        row_total = row_total * jnp.exp(row_top - new_top) + jnp.sum(
            jnp.exp(scores - new_top[:, :, None]), axis=2
        )
        return ((new_top, row_total), None)

    start_top = jnp.full((group_heads, block_tokens), -jnp.inf, jnp.float32)
    start_total = jnp.zeros((group_heads, block_tokens), jnp.float32)
    stats, unused = lax.scan(first_pass, (start_top, start_total), nearby)
    log_total = stats[0] + jnp.log(stats[1])

    def second_pass(query_grad, key_value):
        key_heads = key_value[0].reshape(block_tokens, group_heads, head_dim)
        value_heads = key_value[1].reshape(block_tokens, group_heads, head_dim)
        scores = (
            jnp.einsum("qhd,khd->hqk", query_heads, key_heads, preferred_element_type=jnp.float32)
            * score_scale
        )
        attn_prob = jnp.exp(scores - log_total[:, :, None]).astype(jnp.bfloat16)
        prob_grad = jnp.einsum(
            "qhd,khd->hqk", grad_heads, value_heads, preferred_element_type=jnp.float32
        )
        score_grad = (
            attn_prob.astype(jnp.float32) * (prob_grad - row_delta[:, :, None]) * score_scale
        ).astype(jnp.bfloat16)
        query_grad = query_grad + jnp.einsum(
            "hqk,khd->qhd", score_grad, key_heads, preferred_element_type=jnp.float32
        )
        key_grad = jnp.einsum(
            "hqk,qhd->khd", score_grad, query_heads, preferred_element_type=jnp.float32
        )
        value_grad = jnp.einsum(
            "hqk,qhd->khd", attn_prob, grad_heads, preferred_element_type=jnp.float32
        )
        key_grad = key_grad.astype(jnp.bfloat16).reshape(block_tokens, quarter)
        value_grad = value_grad.astype(jnp.bfloat16).reshape(block_tokens, quarter)
        return (query_grad, jnp.stack([key_grad, value_grad]))

    start_grad = jnp.zeros((block_tokens, group_heads, head_dim), jnp.float32)
    query_block_grad, partials = lax.scan(second_pass, start_grad, nearby)
    summed = partials[0].astype(jnp.float32)
    for slot_index, offset in ((1, -1), (2, 1)):
        summed = summed + shifted(partials[slot_index], "gx", offset).astype(jnp.float32)
    for slot_index, offset in ((3, -2), (4, 2)):
        summed = summed + shifted(partials[slot_index], "gy", offset).astype(jnp.float32)
    for slot_index, offset in ((5, -2), (6, 2)):
        summed = summed + shifted(partials[slot_index], "gz", offset).astype(jnp.float32)
    pair_grads = summed.astype(jnp.bfloat16)
    query_part = query_block_grad.reshape(block_tokens, quarter).astype(jnp.bfloat16)
    block_grads = jnp.concatenate([query_part[None], pair_grads]).reshape(
        3, block_edge, block_edge, block_edge, quarter
    )
    kept_part = lax.dynamic_slice_in_dim(block_grads, y_bit * half_y, half_y, 2)
    sent_part = lax.dynamic_slice_in_dim(block_grads, (1 - y_bit) * half_y, half_y, 2)
    came_part = from_partner(sent_part, "gy", 0)
    by_y = ordered_join(y_bit, kept_part, came_part, 4)
    kept_part = lax.dynamic_slice_in_dim(by_y, z_bit * half_z, half_z, 3)
    sent_part = lax.dynamic_slice_in_dim(by_y, (1 - z_bit) * half_z, half_z, 3)
    came_part = from_partner(sent_part, "gz", 0)
    local_grads = ordered_join(z_bit, kept_part, came_part, 4).reshape(3, local_tokens, width)
    grad_x = transpose_dot(local_grads[0], full_query) + transpose_dot(local_grads[1], full_key)
    grad_x = grad_x + transpose_dot(local_grads[2], full_value)
    grad_x = grad_x.astype(jnp.bfloat16).reshape(features.shape)
    query_term = token_dot(feature_rows, local_grads[0])
    key_term = token_dot(feature_rows, local_grads[1])
    value_term = token_dot(feature_rows, local_grads[2])
    query_shard, key_shard, value_shard, out_shard = (
        lax.psum_scatter(
            query_term.astype(jnp.bfloat16), "gz", scatter_dimension=0, tiled=True
        ).astype(jnp.float32),
        lax.psum_scatter(
            key_term.astype(jnp.bfloat16), "gz", scatter_dimension=0, tiled=True
        ).astype(jnp.float32),
        lax.psum_scatter(
            value_term.astype(jnp.bfloat16), "gz", scatter_dimension=0, tiled=True
        ).astype(jnp.float32),
        lax.psum_scatter(
            out_term.astype(jnp.bfloat16), "gz", scatter_dimension=0, tiled=True
        ).astype(jnp.float32),
    )
    grad_query, grad_key, grad_value, grad_out = lax.psum(
        (query_shard, key_shard, value_shard, out_shard), ("gx", "gy")
    )
    return (grad_x, grad_query, grad_key, grad_value, grad_out)


def solution(mesh):
    return jax.shard_map(
        on_device,
        mesh=mesh,
        in_specs=(
            P("gx", "gy", "gz", None),
            P("gx", "gy", "gz", None),
            P("gx", "gy", "gz", None),
            P("gz", None),
            P("gz", None),
            P("gz", None),
            P("gz", None),
        ),
        out_specs=(
            P("gx", "gy", "gz", None),
            P("gz", None),
            P("gz", None),
            P("gz", None),
            P("gz", None),
        ),
        check_vma=False,
    )
```

profile of v0, /device:TPU:32, one launch (start us, length us, event | category | flops | bytes accessed | tf_op | source)
XLA Modules:
  0.0 691.4 jit_solution(15818092890770009337)
XLA Ops:
  7.2 1.0 reshape.86
  8.2 0.9 reshape.87
  9.2 21.0 %all_gather.12 = bf16[512,512]{1,0:T(8,128)(2,1)S(1)} all-gather(bf16[64,512]{1,0:T(8,128)(2,1)} %param.14), channel_id=1, replica_groups=mesh['gx'=8,'gy'=8,'gz'=8] {'gz'}, dimensions={0}, use_global_device_ids=true | all-gather | bytes 589824 | tf_op jit(solution)/shard_map/all_gather | solution.py:61
  30.4 15.4 %all_gather.13 = bf16[512,512]{1,0:T(8,128)(2,1)S(1)} all-gather(bf16[64,512]{1,0:T(8,128)(2,1)S(1)} %copy-done.5), channel_id=1, replica_groups=mesh['gx'=8,'gy'=8,'gz'=8] {'gz'}, dimensions={0}, use_global_device_ids=true | all-gather | bytes 589824 | tf_op jit(solution)/shard_map/all_gather | solution.py:62
  45.8 0.8 copy-done
  46.9 15.3 %all_gather.14 = bf16[512,512]{1,0:T(8,128)(2,1)S(1)} all-gather(bf16[64,512]{1,0:T(8,128)(2,1)S(1)} %copy-done.6), channel_id=1, replica_groups=mesh['gx'=8,'gy'=8,'gz'=8] {'gz'}, dimensions={0}, use_global_device_ids=true | all-gather | bytes 589824 | tf_op jit(solution)/shard_map/all_gather | solution.py:63
  62.2 0.8 copy-done.2
  63.4 15.5 %all_gather.15 = bf16[512,512]{1,0:T(8,128)(2,1)S(1)} all-gather(bf16[64,512]{1,0:T(8,128)(2,1)S(1)} %copy-done.7), channel_id=1, replica_groups=mesh['gx'=8,'gy'=8,'gz'=8] {'gz'}, dimensions={0}, use_global_device_ids=true | all-gather | bytes 589824 | tf_op jit(solution)/shard_map/all_gather | solution.py:64
  79.7 2.3 collective-permute-start
  82.0 1.2 collective-permute-done
  83.7 3.5 collective-permute-start.1
  87.3 8.3 %collective-permute-done.1 = bf16[5,8,4,8,128]{4,3,2,1,0:T(8,128)(2,1)S(1)} collective-permute-done((bf16[5,8,4,8,128]{4,3,2,1,0:T(8,128)(2,1)S(1)}, bf16[5,8,4,8,128]{4,3,2,1,0:T(8,128)(2,1)S(1)}, u32[]{:S(2)}, u32[]{:S(2)}) %collective-permute-start.1) | collective-permute-done | bytes 327712 | tf_op jit(solution)/shard_map/ppermute | solution.py:18
  96.1 5.2 collective-permute-start.7
  101.3 1.9 collective-permute-start.6
  103.3 4.7 collective-permute-start.5
  107.9 2.2 collective-permute-start.3
  110.1 3.6 collective-permute-start.2
  115.0 0.7 constant_dynamic-update-slice_fusion.5
  116.2 4.3 collective-permute-done.2
  120.5 1.9 collective-permute-start.4
  122.4 1.7 bitcast_dynamic-update-slice_fusion.5
  124.1 0.7 bitcast_dynamic-update-slice_fusion.4
  124.8 5.2 collective-permute-done.4
  130.0 0.7 bitcast_dynamic-update-slice_fusion.3
  130.7 0.7 bitcast_dynamic-update-slice_fusion.2
  132.1 0.7 bitcast_dynamic-update-slice_fusion
  132.9 2.7 copy.42
  135.6 6.7 while.26
  142.4 22.7 %while.27 = (s32[]{:T(128)}, f32[512,2,64]{0,2,1:T(8,128)S(1)}, bf16[7,2,512,128]{3,2,1,0:T(8,128)(2,1)}, bf16[7,2,512,128]{2,3,1,0:T(8,128)(2,1)S(1)}, bf16[512...) while((s32[]{:T(128)}, f32[512,2,64]{0,2,1:T(8,128)S(1)}, ...), condition=%wide.region_6.7_spmd.clone, body=%wide.region_5.6_spmd.clone.sunk | while | flops 340131840 | bytes 10100887 | solution.py:151
  144.9 0.7 constant_dynamic-update-slice_fusion.7
  148.1 0.7 constant_dynamic-update-slice_fusion.7
  154.6 0.7 constant_dynamic-update-slice_fusion.7
  157.9 0.7 constant_dynamic-update-slice_fusion.7
  161.1 0.7 constant_dynamic-update-slice_fusion.7
  164.3 0.7 constant_dynamic-update-slice_fusion.7
  165.0 1.4 slice_bitcast_fusion.5
  166.5 1.9 collective-permute-start.8
  168.4 5.8 collective-permute-start.12
  174.2 1.9 collective-permute-start.11
  176.1 5.1 collective-permute-start.10
  181.3 3.9 collective-permute-start.9
  185.2 1.9 collective-permute-start.13
  187.5 3.3 collective-permute-done.9
  190.8 7.2 %collective-permute-done.13 = bf16[2,512,128]{2,1,0:T(8,128)(2,1)} collective-permute-done((bf16[2,512,128]{2,1,0:T(8,128)(2,1)S(1)}, bf16[2,512,128]{2,1,0:T(8,128)(2,1)}, u32[]{:S(2)}, u32[]{:S(2)}) %collective-permute-start.13) | collective-permute-done | bytes 262176 | tf_op jit(solution)/shard_map/ppermute | solution.py:24
  198.0 1.4 fusion.15
  199.4 4.3 collective-permute-start.14
  203.7 2.2 fusion.5
  206.0 1.4 collective-permute-done.14
  207.5 2.1 collective-permute-start.15
  209.7 1.2 collective-permute-done.15
  211.7 1.0 copy.62
  213.1 1.0 copy.60
  214.6 1.0 copy.58
  215.6 26.6 %reduce-scatter.11.cloned.1.call-done = bf16[64,512]{1,0:T(8,128)(2,1)} async-done(((bf16[512,512]{1,0:T(8,128)(2,1)}), bf16[64,512]{1,0:T(8,128)(2,1)}) %reduce-scatter.11.cloned.1.call-update) | async-done | bytes 65552 | tf_op jit(solution)/shard_map/reduce_scatter | solution.py:188
  243.9 40.2 %reduce-scatter.17.cloned.1.call-done = bf16[64,512]{1,0:T(8,128)(2,1)} async-done(((bf16[512,512]{1,0:T(8,128)(2,1)}), bf16[64,512]{1,0:T(8,128)(2,1)}) %reduce-scatter.17.cloned.1.call-update) | async-done | bytes 65552
  284.1 1.0 copy.63
  285.0 40.7 %reduce-scatter.15.cloned.1.call-done = bf16[64,512]{1,0:T(8,128)(2,1)} async-done(((bf16[512,512]{1,0:T(8,128)(2,1)}), bf16[64,512]{1,0:T(8,128)(2,1)}) %reduce-scatter.15.cloned.1.call-update) | async-done | bytes 65552
  325.8 1.0 copy.61
  326.7 40.6 %reduce-scatter.13.cloned.1.call-done = bf16[64,512]{1,0:T(8,128)(2,1)} async-done(((bf16[512,512]{1,0:T(8,128)(2,1)}), bf16[64,512]{1,0:T(8,128)(2,1)}) %reduce-scatter.13.cloned.1.call-update) | async-done | bytes 65552
  367.3 1.0 copy.59
  368.3 314.3 %all-reduce.2 = (f32[64,512]{0,1:T(8,128)S(1)}, f32[64,512]{0,1:T(8,128)S(1)}, f32[64,512]{0,1:T(8,128)S(1)}, f32[64,512]{1,0:T(8,128)}) all-reduce(bf16[64,512]{0,1:T(8,128)(2,1)S(1)} %copy.59, bf16[64,512]{0,1:T(8,128)(2,1)S(1)} %copy.61, bf16[64,512]{0,1:T(8,128)(2,1)S(1)} %copy.63, ...), channel_id=1, replica_groups=mesh['gx'=8,'gy'=8,'gz'=8] {'gx','gy'}, use_global_device_ids=true, to_apply=%region_8.9 | all-reduce | flops 131072 | bytes 786432 | tf_op jit(solution)/shard_map/psum | solution.py:192
  682.5 0.8 copy.54
  683.3 0.8 copy.55
  684.1 0.8 copy.56
  (181 shorter events, 33.2 us)
Async XLA Ops:
  7.2 23.3 %copy-start.5 = (bf16[64,512]{1,0:T(8,128)(2,1)S(1)}, bf16[64,512]{1,0:T(8,128)(2,1)}, u32[]{:S(2)}) copy-start(bf16[64,512]{1,0:T(8,128)(2,1)} %param.15) | copy-start | bytes 196612
  7.2 235.0 %reduce-scatter.11.cloned.1.call-start = ((), (), s32[]{:S(2)}) async-start(), calls=%async_computation.4 | async-start | bytes 589824 | tf_op jit(solution)/shard_map/reduce_scatter | solution.py:188
  7.2 39.7 %copy-start.6 = (bf16[64,512]{1,0:T(8,128)(2,1)S(1)}, bf16[64,512]{1,0:T(8,128)(2,1)}, u32[]{:S(2)}) copy-start(bf16[64,512]{1,0:T(8,128)(2,1)} %param.16) | copy-start | bytes 196612
  30.4 33.0 %copy-start.7 = (bf16[64,512]{1,0:T(8,128)(2,1)S(1)}, bf16[64,512]{1,0:T(8,128)(2,1)}, u32[]{:S(2)}) copy-start(bf16[64,512]{1,0:T(8,128)(2,1)} %param.17) | copy-start | bytes 196612
  45.8 0.8 copy-start
  62.2 0.8 copy-start.2
  63.0 16.4 %copy-start.4 = (bf16[8,4,4,512]{3,2,1,0:T(4,128)(2,1)S(1)}, bf16[8,4,4,512]{3,2,1,0:T(4,128)(2,1)}, u32[]{:S(2)}) copy-start(bf16[8,4,4,512]{3,2,1,0:T(4,128)(2,1)} %param.13) | copy-start | bytes 393220
  79.7 3.5 collective-permute-start
  83.7 11.9 %collective-permute-start.1 = (bf16[5,8,4,8,128]{4,3,2,1,0:T(8,128)(2,1)S(1)}, bf16[5,8,4,8,128]{4,3,2,1,0:T(8,128)(2,1)S(1)}, u32[]{:S(2)}, u32[]{:S(2)}) collective-permute-start(bf16[5,8,4,8,128]{4,3,2,1,0:T(8,128)(2,1)S(1)} %fusion.16), channel_id=1, source_target_pairs={{0,8},{8,0},{16,24},{24,16},{32,40},{40,32},{48,56},{56,48},{1,9},... | collective-permute-start | bytes 983048 | tf_op jit(solution)/shard_map/ppermute | solution.py:18
  96.1 36.1 %collective-permute-start.7 = (bf16[2,512,128]{2,1,0:T(8,128)(2,1)S(1)}, bf16[2,512,128]{2,1,0:T(8,128)(2,1)S(1)}, u32[]{:S(2)}, u32[]{:S(2)}) collective-permute-start(bf16[2,512,128]{2,1,0:T(8,128)(2,1)S(1)} %bitcast.160), channel_id=1, source_target_pairs={{0,6},{1,7},{2,0},{3,1},{4,2},{5,3},{6,4},{7,5},{8,14},{9,15},{10,... | collective-permute-start | bytes 786440 | tf_op jit(solution)/shard_map/ppermute | solution.py:24
  101.3 30.1 %collective-permute-start.6 = (bf16[2,512,128]{2,1,0:T(8,128)(2,1)S(1)}, bf16[2,512,128]{2,1,0:T(8,128)(2,1)S(1)}, u32[]{:S(2)}, u32[]{:S(2)}) collective-permute-start(bf16[2,512,128]{2,1,0:T(8,128)(2,1)S(1)} %bitcast.161), channel_id=1, source_target_pairs={{0,2},{1,3},{2,4},{3,5},{4,6},{5,7},{6,0},{7,1},{8,10},{9,11},{10,... | collective-permute-start | bytes 786440 | tf_op jit(solution)/shard_map/ppermute | solution.py:24
  103.3 27.4 %collective-permute-start.5 = (bf16[2,512,128]{2,1,0:T(8,128)(2,1)S(1)}, bf16[2,512,128]{2,1,0:T(8,128)(2,1)S(1)}, u32[]{:S(2)}, u32[]{:S(2)}) collective-permute-start(bf16[2,512,128]{2,1,0:T(8,128)(2,1)S(1)} %bitcast.162), channel_id=1, source_target_pairs={{0,48},{8,56},{16,0},{24,8},{32,16},{40,24},{48,32},{56,40},{1,49}... | collective-permute-start | bytes 786440 | tf_op jit(solution)/shard_map/ppermute | solution.py:24
  107.9 16.2 %collective-permute-start.3 = (bf16[2,512,128]{2,1,0:T(8,128)(2,1)S(1)}, bf16[2,512,128]{2,1,0:T(8,128)(2,1)S(1)}, u32[]{:S(2)}, u32[]{:S(2)}) collective-permute-start(bf16[2,512,128]{2,1,0:T(8,128)(2,1)S(1)} %bitcast.163), channel_id=1, source_target_pairs={{0,448},{64,0},{128,64},{192,128},{256,192},{320,256},{384,320},{4... | collective-permute-start | bytes 786440 | tf_op jit(solution)/shard_map/ppermute | solution.py:24
  110.1 10.4 %collective-permute-start.2 = (bf16[2,512,128]{2,1,0:T(8,128)(2,1)S(1)}, bf16[2,512,128]{2,1,0:T(8,128)(2,1)}, u32[]{:S(2)}, u32[]{:S(2)}) collective-permute-start(bf16[2,512,128]{2,1,0:T(8,128)(2,1)S(1)} %bitcast.164), channel_id=1, source_target_pairs={{0,64},{64,128},{128,192},{192,256},{256,320},{320,384},{384,448},... | collective-permute-start | bytes 786440 | tf_op jit(solution)/shard_map/ppermute | solution.py:24
  120.5 9.5 %collective-permute-start.4 = (bf16[2,512,128]{2,1,0:T(8,128)(2,1)S(1)}, bf16[2,512,128]{2,1,0:T(8,128)(2,1)S(1)}, u32[]{:S(2)}, u32[]{:S(2)}) collective-permute-start(bf16[2,512,128]{2,1,0:T(8,128)(2,1)S(1)} %bitcast.166), channel_id=1, source_target_pairs={{0,16},{8,24},{16,32},{24,40},{32,48},{40,56},{48,0},{56,8},{1,17}... | collective-permute-start | bytes 786440 | tf_op jit(solution)/shard_map/ppermute | solution.py:24
  166.5 18.7 %collective-permute-start.8 = (bf16[2,512,128]{2,1,0:T(8,128)(2,1)S(1)}, bf16[2,512,128]{2,1,0:T(8,128)(2,1)S(1)}, u32[]{:S(2)}, u32[]{:S(2)}) collective-permute-start(bf16[2,512,128]{2,1,0:T(8,128)(2,1)S(1)} %get-tuple-element.200), channel_id=1, source_target_pairs={{0,448},{64,0},{128,64},{192,128},{256,192},{320,256},{384,320},{4... | collective-permute-start | bytes 786440 | tf_op jit(solution)/shard_map/ppermute | solution.py:24
  168.4 19.1 %collective-permute-start.12 = (bf16[2,512,128]{2,1,0:T(8,128)(2,1)S(1)}, bf16[2,512,128]{2,1,0:T(8,128)(2,1)S(1)}, u32[]{:S(2)}, u32[]{:S(2)}) collective-permute-start(bf16[2,512,128]{2,1,0:T(8,128)(2,1)S(1)} %get-tuple-element.201), channel_id=1, source_target_pairs={{0,6},{1,7},{2,0},{3,1},{4,2},{5,3},{6,4},{7,5},{8,14},{9,15},{10,... | collective-permute-start | bytes 786440 | tf_op jit(solution)/shard_map/ppermute | solution.py:24
  174.2 13.3 %collective-permute-start.11 = (bf16[2,512,128]{2,1,0:T(8,128)(2,1)S(1)}, bf16[2,512,128]{2,1,0:T(8,128)(2,1)S(1)}, u32[]{:S(2)}, u32[]{:S(2)}) collective-permute-start(bf16[2,512,128]{2,1,0:T(8,128)(2,1)S(1)} %get-tuple-element.202), channel_id=1, source_target_pairs={{0,16},{8,24},{16,32},{24,40},{32,48},{40,56},{48,0},{56,8},{1,17}... | collective-permute-start | bytes 786440 | tf_op jit(solution)/shard_map/ppermute | solution.py:24
  176.1 11.4 %collective-permute-start.10 = (bf16[2,512,128]{2,1,0:T(8,128)(2,1)S(1)}, bf16[2,512,128]{2,1,0:T(8,128)(2,1)S(1)}, u32[]{:S(2)}, u32[]{:S(2)}) collective-permute-start(bf16[2,512,128]{2,1,0:T(8,128)(2,1)S(1)} %get-tuple-element.203), channel_id=1, source_target_pairs={{0,48},{8,56},{16,0},{24,8},{32,16},{40,24},{48,32},{56,40},{1,49}... | collective-permute-start | bytes 786440 | tf_op jit(solution)/shard_map/ppermute | solution.py:24
  181.3 9.6 %collective-permute-start.9 = (bf16[2,512,128]{2,1,0:T(8,128)(2,1)S(1)}, bf16[2,512,128]{2,1,0:T(8,128)(2,1)}, u32[]{:S(2)}, u32[]{:S(2)}) collective-permute-start(bf16[2,512,128]{2,1,0:T(8,128)(2,1)S(1)} %get-tuple-element.204), channel_id=1, source_target_pairs={{0,64},{64,128},{128,192},{192,256},{256,320},{320,384},{384,448},... | collective-permute-start | bytes 786440 | tf_op jit(solution)/shard_map/ppermute | solution.py:24
  185.2 12.8 %collective-permute-start.13 = (bf16[2,512,128]{2,1,0:T(8,128)(2,1)S(1)}, bf16[2,512,128]{2,1,0:T(8,128)(2,1)}, u32[]{:S(2)}, u32[]{:S(2)}) collective-permute-start(bf16[2,512,128]{2,1,0:T(8,128)(2,1)S(1)} %get-tuple-element.205), channel_id=1, source_target_pairs={{0,2},{1,3},{2,4},{3,5},{4,6},{5,7},{6,0},{7,1},{8,10},{9,11},{10,... | collective-permute-start | bytes 786440 | tf_op jit(solution)/shard_map/ppermute | solution.py:24
  199.4 7.9 %collective-permute-start.14 = (bf16[3,8,4,8,128]{4,3,2,1,0:T(8,128)(2,1)S(1)}, bf16[3,8,4,8,128]{4,3,2,1,0:T(8,128)(2,1)S(1)}, u32[]{:S(2)}, u32[]{:S(2)}) collective-permute-start(bf16[3,8,4,8,128]{4,3,2,1,0:T(8,128)(2,1)S(1)} %fusion.19), channel_id=1, source_target_pairs={{0,8},{8,0},{16,24},{24,16},{32,40},{40,32},{48,56},{56,48},{1,9},... | collective-permute-start | bytes 589832 | tf_op jit(solution)/shard_map/ppermute | solution.py:18
  205.9 78.2 %reduce-scatter.17.cloned.1.call-start = ((), (), s32[]{:S(2)}) async-start(), calls=%async_computation.7 | async-start | bytes 589824
  207.5 3.3 collective-permute-start.15
  212.7 113.0 %reduce-scatter.15.cloned.1.call-start = ((), (), s32[]{:S(2)}) async-start(), calls=%async_computation.6 | async-start | bytes 589824
  214.2 28.4 %copy-start.1 = (bf16[512,512]{1,0:T(8,128)(2,1)S(1)}, bf16[512,512]{1,0:T(8,128)(2,1)}, u32[]{:S(2)}) copy-start(bf16[512,512]{1,0:T(8,128)(2,1)} %copy-done) | copy-start | bytes 1572868
  214.2 153.1 %reduce-scatter.13.cloned.1.call-start = ((), (), s32[]{:S(2)}) async-start(), calls=%async_computation.5 | async-start | bytes 589824
  214.6 28.3 %copy-start.3 = (bf16[512,512]{1,0:T(8,128)(2,1)S(1)}, bf16[512,512]{1,0:T(8,128)(2,1)}, u32[]{:S(2)}) copy-start(bf16[512,512]{1,0:T(8,128)(2,1)} %copy-done.2) | copy-start | bytes 1572868
  242.2 126.1 %copy-start.8 = (bf16[64,512]{1,0:T(8,128)(2,1)S(1)}, bf16[64,512]{1,0:T(8,128)(2,1)}, u32[]{:S(2)}) copy-start(bf16[64,512]{1,0:T(8,128)(2,1)} %reduce-scatter.11.cloned.1.call-done) | copy-start | bytes 196612
Sparse Core Ops, SparseCore 0:
  206.0 36.1 reduce-scatter.10
  245.0 39.0 reduce-scatter.16
  286.9 38.8 reduce-scatter.14
  328.4 38.8 reduce-scatter.12
where the time goes:
time: 692 us; the launch traced here: 691 us
  blocking collectives  381 us (55%)
  waiting for transfers between devices  180 us (26%)
  starting transfers between devices  52.5 us (8%)
  local copies, waits for them, and re-layouts  31.1 us (4%)
  matrix products  24.3 us (4%)
  between operations  14.5 us (2%)
    psum x1, blocking collectives, on_device(): lax.psum((query_shard, key_shard, value_shard, out_shard), ('gx', 'gy'))  314 us
    unnamed x7, waiting for transfers between devices  122 us
    ppermute x12, starting transfers between devices, shifted(): return lax.ppermute(value, axis, pairs)  40.2 us
    reduce_scatter x1, waiting for transfers between devices, on_device(): lax.psum_scatter(out_term.astype(jnp.bfloat16), 'gz', scatter_dimension=0...  26.6 us
    all_gather x1, blocking collectives, on_device(): lax.all_gather(w_query, 'gz', axis=0, tiled=True)  21 us
    ppermute x12, waiting for transfers between devices, shifted(): return lax.ppermute(value, axis, pairs)  20 us
    unnamed x41, local copies, waits for them, and re-layouts  18.5 us
    all_gather x1, blocking collectives, on_device(): lax.all_gather(w_out, 'gz', axis=0, tiled=True)  15.5 us
  transfers between devices with their start and end apart: 20, of which 12 were waited for; matrix products, arithmetic and copies ran while one was open for 3% of the time, Pallas kernels for 0%

commit v1 on v0

v1 whole, which is shorter than its diff:
```python
import functools
import math

import jax
import jax.numpy as jnp
from jax import lax
from jax.experimental import pallas as pl
from jax.experimental.pallas import tpu as pltpu
from jax.sharding import PartitionSpec as P

HEADS = 8
MESH = pl.DeviceIdType.MESH
STEPS = (("gx", 1), ("gx", -1), ("gy", 2), ("gy", -2), ("gz", 2), ("gz", -2))
BF16 = jnp.bfloat16
F32 = jnp.float32


def remote(src, dst, send, recv, device):
    return pltpu.make_async_remote_copy(
        src_ref=src, dst_ref=dst, send_sem=send, recv_sem=recv, device_id=device, device_id_type=MESH
    )


def greet(devices):
    barrier = pltpu.get_barrier_semaphore()
    for device in devices:
        pl.semaphore_signal(barrier, inc=1, device_id=device, device_id_type=MESH)
    pl.semaphore_wait(barrier, len(devices))


def ring(axis, index, step):
    return {axis: lax.rem(index + step + 8, 8)}


def gather_kernel(
    f_ref, g_ref, a_ref, wq_ref, wk_ref, wv_ref, wo_ref,
    fb_ref, gb_ref, ab_ref, w3_ref, wob_ref,
    bsend, brecv, wsend, wrecv, osend, orecv,
):
    gy, gz = lax.axis_index("gy"), lax.axis_index("gz")
    y_bit, z_bit = lax.rem(gy, 2), lax.rem(gz, 2)
    pair_z = {"gz": gz + 1 - 2 * z_bit}
    pair_y = {"gy": gy + 1 - 2 * y_bit}
    slot = 2 * y_bit + z_bit
    slot_y = 2 * (1 - y_bit) + z_bit
    greet([ring("gz", gz, d) for d in range(1, 8)] + [pair_y])
    trios = ((f_ref, fb_ref), (g_ref, gb_ref), (a_ref, ab_ref))
    to_y, to_z, onward = [], [], []
    for i, (src, dst) in enumerate(trios):
        to_y.append(remote(src, dst.at[slot], bsend.at[0, i], brecv.at[0, i], pair_y))
        to_z.append(remote(src, dst.at[slot], bsend.at[1, i], brecv.at[1, i], pair_z))
        to_y[-1].start()
        to_z[-1].start()
    weights = (wq_ref, wk_ref, wv_ref)
    rows = pl.ds(pl.multiple_of(gz * 64, 64), 64)
    weight_copies = []
    for d in (4, 3, 5, 2, 6, 1, 7):
        target = lax.rem(gz + d, 8)
        columns = pl.ds(pl.multiple_of(lax.rem(target, 2) * 256 + y_bit * 128, 128), 128)
        for i, w_ref in enumerate(weights):
            copy = remote(
                w_ref.at[:, columns], w3_ref.at[i, rows], wsend.at[d - 1, i], wrecv.at[d - 1, i], {"gz": target}
            )
            copy.start()
            weight_copies.append(copy)
    half = lax.rem(gz, 2)
    out_core = lax.div(gz, 4)
    out_from = lax.rem(lax.div(gz, 2), 2) == y_bit
    out_rows = pl.ds(pl.multiple_of(half * 64, 64), 64)

    def out_copy(zh):
        return remote(wo_ref, wob_ref.at[out_rows], osend.at[zh], orecv.at[half], {"gz": 2 * zh + out_core})

    for zh in range(4):

        @pl.when(jnp.logical_and(out_from, 2 * zh + out_core != gz))
        def _():
            out_copy(zh).start()

    columns = pl.ds(pl.multiple_of(z_bit * 256 + y_bit * 128, 128), 128)
    for i, w_ref in enumerate(weights):
        w3_ref[i, rows] = w_ref[:, columns]
    for src, dst in trios:
        dst[slot] = src[...]
    for i, (src, dst) in enumerate(trios):
        to_y[i].wait_recv()
        onward.append(remote(dst.at[slot_y], dst.at[slot_y], bsend.at[2, i], brecv.at[2, i], pair_z))
        onward[-1].start()
    for s in range(2):
        source = 4 * z_bit + 2 * y_bit + s

        @pl.when(source != gz)
        def _():
            remote(wo_ref, wob_ref.at[pl.ds(s * 64, 64)], osend.at[0], orecv.at[s], {"gz": source}).wait_recv()

        @pl.when(source == gz)
        def _():
            wob_ref[pl.ds(s * 64, 64)] = wo_ref[...]

    for copy in weight_copies:
        copy.wait()
    for zh in range(4):

        @pl.when(jnp.logical_and(out_from, 2 * zh + out_core != gz))
        def _():
            out_copy(zh).wait_send()

    for i in range(3):
        to_y[i].wait_send()
        to_z[i].wait()
        onward[i].wait()


def swap_kernel(sign, src_ref, dst_ref, send, recv):
    index = {axis: lax.axis_index(axis) for axis in ("gx", "gy", "gz")}
    greet([ring(axis, index[axis], step) for axis, step in STEPS])
    copies = []
    for k in (4, 5, 0, 1, 2, 3):
        axis, step = STEPS[k]
        src = src_ref.at[k] if sign < 0 else src_ref
        copies.append(remote(src, dst_ref.at[k], send.at[k], recv.at[k], ring(axis, index[axis], sign * step)))
        copies[-1].start()
    for copy in copies:
        copy.wait()


def reduce_kernel(
    t_ref, g_ref, h_ref, gx_ref,
    xr, s1, yr, s2, zr, u, gr,
    xsend, xrecv, ysend, yrecv, zsend, zrecv, usend, urecv, hsend, hrecv, gsend, grecv,
):
    gx, gy, gz = (lax.axis_index(axis) for axis in ("gx", "gy", "gz"))
    y_bit, z_bit = lax.rem(gy, 2), lax.rem(gz, 2)
    x = lax.div(gy, 2)
    other_z, other_y = gz + 1 - 2 * z_bit, gy + 1 - 2 * y_bit
    greet(
        [ring("gy", gy, d) for d in range(1, 8)]
        + [ring("gx", gx, d) for d in range(1, 8)]
        + [ring("gz", gz, d) for d in range(1, 8)]
        + [{"gy": other_y, "gz": other_z}]
    )

    def run(copies):
        for copy in copies:
            copy.start()
        return copies

    def join(copies):
        for copy in copies:
            copy.wait()

    x_copies = []
    for d in (2, 1, 3):
        target = lax.rem(x + d, 4)
        x_copies.append(
            remote(t_ref.at[target], xr.at[d - 1], xsend.at[d - 1], xrecv.at[d - 1], {"gy": 2 * target + y_bit})
        )
    run(x_copies)
    parts = (
        (2 * (1 - y_bit) + 1 - z_bit, {"gy": other_y, "gz": other_z}),
        (2 * (1 - y_bit) + z_bit, {"gy": other_y}),
        (2 * y_bit + 1 - z_bit, {"gz": other_z}),
    )
    g_copies = run(
        [remote(g_ref.at[part], gr.at[k], gsend.at[k], grecv.at[k], dev) for k, (part, dev) in enumerate(parts)]
    )
    join(x_copies)
    total = t_ref[x].astype(F32)
    for d in range(3):
        total = total + xr[d].astype(F32)
    s1[...] = total.astype(BF16)
    y_copies = []
    for d in (4, 3, 5, 2, 6, 1, 7):
        target = lax.rem(gx + d, 8)
        y_copies.append(remote(s1.at[target], yr.at[d - 1], ysend.at[d - 1], yrecv.at[d - 1], {"gx": target}))
    run(y_copies)
    join(y_copies)
    total = s1[gx].astype(F32)
    for d in range(7):
        total = total + yr[d].astype(F32)
    s2[...] = total.reshape(8, 8, 128)
    z_copies = []
    for d in (4, 3, 5, 2, 6, 1, 7):
        target = lax.rem(gz + d, 8)
        z_copies.append(remote(s2.at[target], zr.at[gz], zsend.at[d - 1], zrecv.at[d - 1], {"gz": target}))
    run(z_copies)
    zr[gz] = s2[gz]
    join(z_copies)
    lower = zr[0] + zr[2] + zr[4] + zr[6]
    upper = zr[1] + zr[3] + zr[5] + zr[7]
    u[gx] = jnp.concatenate([lower, upper], axis=0).astype(BF16)
    u_copies = []
    for d in (4, 3, 5, 2, 6, 1, 7):
        u_copies.append(remote(u.at[gx], u.at[gx], usend.at[d - 1], urecv.at[d - 1], ring("gx", gx, d)))
    run(u_copies)
    join(g_copies)
    total = g_ref[2 * y_bit + z_bit].astype(F32)
    for k in range(3):
        total = total + gr[k].astype(F32)
    gx_ref[...] = total.astype(BF16)
    join(u_copies)
    h_copies = []
    for d in (4, 3, 5, 2, 6, 1, 7):
        h_copies.append(remote(u, h_ref.at[gy], hsend.at[d - 1], hrecv.at[d - 1], ring("gy", gy, d)))
    run(h_copies)
    h_ref[gy] = u[...]
    join(h_copies)


def vmem(count):
    return [pl.BlockSpec(memory_space=pltpu.VMEM)] * count


def dma(*shape):
    return pltpu.SemaphoreType.DMA(shape)


def call(kernel, number, shapes, scratch, *operands):
    return pl.pallas_call(
        kernel,
        out_shape=[jax.ShapeDtypeStruct(shape, BF16) for shape in shapes],
        in_specs=vmem(len(operands)),
        out_specs=vmem(len(shapes)),
        scratch_shapes=scratch,
        compiler_params=pltpu.CompilerParams(collective_id=number, has_side_effects=True),
    )(*operands)


def transpose_dot(left, right):
    return lax.dot_general(left, right, (((1,), (1,)), ((), ())), preferred_element_type=F32)


def token_dot(left, right):
    return lax.dot_general(left, right, (((0,), (0,)), ((), ())), preferred_element_type=F32)


def dot(left, right):
    return jnp.dot(left, right, preferred_element_type=F32)


def attention(query, grad, row_delta, nearby):
    tokens, quarter = query.shape
    head_dim = 64
    group_heads = quarter // head_dim
    score_scale = 1.0 / math.sqrt(head_dim)
    query_heads = query.reshape(tokens, group_heads, head_dim)
    grad_heads = grad.reshape(tokens, group_heads, head_dim)

    def first_pass(carry, key_value):
        row_top, row_total = carry
        key_heads = key_value[0].reshape(tokens, group_heads, head_dim)
        scores = jnp.einsum("qhd,khd->hqk", query_heads, key_heads, preferred_element_type=F32) * score_scale
        new_top = jnp.maximum(row_top, jnp.max(scores, axis=2))
        row_total = row_total * jnp.exp(row_top - new_top) + jnp.sum(jnp.exp(scores - new_top[:, :, None]), axis=2)
        return ((new_top, row_total), None)

    start_top = jnp.full((group_heads, tokens), -jnp.inf, F32)
    start_total = jnp.zeros((group_heads, tokens), F32)
    stats, unused = lax.scan(first_pass, (start_top, start_total), nearby)
    log_total = stats[0] + jnp.log(stats[1])

    def second_pass(query_grad, key_value):
        key_heads = key_value[0].reshape(tokens, group_heads, head_dim)
        value_heads = key_value[1].reshape(tokens, group_heads, head_dim)
        scores = jnp.einsum("qhd,khd->hqk", query_heads, key_heads, preferred_element_type=F32) * score_scale
        prob = jnp.exp(scores - log_total[:, :, None]).astype(BF16)
        prob_grad = jnp.einsum("qhd,khd->hqk", grad_heads, value_heads, preferred_element_type=F32)
        score_grad = (prob.astype(F32) * (prob_grad - row_delta[:, :, None]) * score_scale).astype(BF16)
        query_grad = query_grad + jnp.einsum("hqk,khd->qhd", score_grad, key_heads, preferred_element_type=F32)
        key_grad = jnp.einsum("hqk,qhd->khd", score_grad, query_heads, preferred_element_type=F32)
        value_grad = jnp.einsum("hqk,qhd->khd", prob, grad_heads, preferred_element_type=F32)
        key_grad = key_grad.astype(BF16).reshape(tokens, quarter)
        value_grad = value_grad.astype(BF16).reshape(tokens, quarter)
        return (query_grad, jnp.stack([key_grad, value_grad]))

    start_grad = jnp.zeros((tokens, group_heads, head_dim), F32)
    query_grad, partials = lax.scan(second_pass, start_grad, nearby)
    return query_grad.reshape(tokens, quarter).astype(BF16), partials


def on_device(features, grad_y, attn_out, w_query, w_key, w_value, w_out):
    width = features.shape[3]
    local = features.shape[0] * features.shape[1] * features.shape[2]
    tokens = 4 * local
    quarter = width // 4
    feature_rows = features.reshape(local, width)
    dy_rows = grad_y.reshape(local, width)
    saved_rows = attn_out.reshape(local, width)
    fb, gb, ab, w3, wo = call(
        gather_kernel,
        0,
        [(4, local, width)] * 3 + [(3, width, quarter), (quarter, width)],
        [dma(3, 3), dma(3, 3), dma(7, 3), dma(7, 3), dma(4), dma(2)],
        feature_rows, dy_rows, saved_rows, w_query, w_key, w_value, w_out,
    )
    fb, gb, ab = (block.reshape(tokens, width) for block in (fb, gb, ab))
    start = (lax.axis_index("gz") % 2) * (2 * quarter) + (lax.axis_index("gy") % 2) * quarter
    own_gb = lax.dynamic_slice_in_dim(gb, start, quarter, 1)
    own_ab = lax.dynamic_slice_in_dim(ab, start, quarter, 1)
    query, key, value = (dot(fb, w3[i]).astype(BF16) for i in range(3))
    grad = transpose_dot(gb, wo).astype(BF16)
    own_pair = jnp.stack([key, value])
    (near,) = call(
        functools.partial(swap_kernel, 1), 1, [(6, 2, tokens, quarter)], [dma(6), dma(6)], own_pair
    )
    products = grad.astype(F32) * own_ab.astype(F32)
    row_delta = jnp.sum(products.reshape(tokens, 2, quarter // 2), axis=2).T
    query_grad, partials = attention(query, grad, row_delta, jnp.concatenate([own_pair[None], near]))
    (back,) = call(
        functools.partial(swap_kernel, -1), 2, [(6, 2, tokens, quarter)], [dma(6), dma(6)], partials[1:]
    )
    pair_grads = (partials[0].astype(F32) + jnp.sum(back.astype(F32), axis=0)).astype(BF16)
    grads = (query_grad, pair_grads[0], pair_grads[1])
    partial_x = sum(transpose_dot(grads[i], w3[i]) for i in range(3))
    partial_x = partial_x.astype(BF16).reshape(4, local, width)
    terms = jnp.stack([token_dot(fb, part) for part in grads] + [token_dot(ab, own_gb)])
    terms = terms.astype(BF16).reshape(4, 8, 8, 8, quarter).transpose(0, 2, 1, 3, 4)
    terms = terms.reshape(4, 8, 64, quarter)
    rows, grad_x = call(
        reduce_kernel,
        3,
        [(8, 8, 16, quarter), (local, width)],
        [
            pltpu.VMEM((3, 8, 64, quarter), BF16),
            pltpu.VMEM((8, 64, quarter), BF16),
            pltpu.VMEM((7, 64, quarter), BF16),
            pltpu.VMEM((8, 8, quarter), F32),
            pltpu.VMEM((8, 8, quarter), F32),
            pltpu.VMEM((8, 16, quarter), BF16),
            pltpu.VMEM((3, local, width), BF16),
            dma(3), dma(3), dma(7), dma(7), dma(7), dma(7), dma(7), dma(7), dma(7), dma(7), dma(3), dma(3),
        ],
        terms, partial_x,
    )
    rows = rows.astype(F32).reshape(4, 2, 8, 2, 8, quarter).transpose(0, 2, 4, 3, 1, 5).reshape(4, 64, width)
    return (grad_x.reshape(features.shape), rows[0], rows[1], rows[2], rows[3])


def solution(mesh):
    token_spec = P("gx", "gy", "gz", None)
    row_spec = P("gz", None)
    return jax.shard_map(
        on_device,
        mesh=mesh,
        in_specs=(token_spec,) * 3 + (row_spec,) * 4,
        out_specs=(token_spec,) + (row_spec,) * 4,
        check_vma=False,
    )
```

time: 692 us -> 171 us (0.25)
  the two profiles are of different devices: /device:TPU:32 before, /device:TPU:1 now
where the time goes in v1:
time: 171 us; the launch traced here: 170 us
  Pallas kernels  109 us (64%)
  matrix products  27.6 us (16%)
  local copies, waits for them, and re-layouts  21.1 us (12%)
  other arithmetic  11.2 us (7%)
    pallas_call x4, Pallas kernels, call(): pl.pallas_call(kernel, out_shape=[jax.ShapeDtypeStruct(shape, BF16) for s...  109 us
    dynamic_update_slice x14, local copies, waits for them, and re-layouts, attention(): query_grad, partials = lax.scan(second_pass, start_grad, nearby)  6.24 us
    dot_general x4, matrix products, transpose_dot(): lax.dot_general(left, right, (((1,), (1,)), ((), ())), preferred_element_...  4.22 us
    dot_general x7, matrix products, second_pass(): jnp.einsum('qhd,khd->hqk', query_heads, key_heads, preferred_element_type...  3.79 us
    dot_general x7, matrix products, second_pass(): jnp.einsum('qhd,khd->hqk', grad_heads, value_heads, preferred_element_typ...  3.69 us
    dot_general x7, matrix products, first_pass(): jnp.einsum('qhd,khd->hqk', query_heads, key_heads, preferred_element_type...  3.51 us

profile of v1, /device:TPU:1, one launch (start us, length us, event | category | flops | bytes accessed | tf_op | source)
XLA Modules:
  0.0 170.1 jit_solution(13633831614701104936)
XLA Ops:
  0.7 1.6 reshape.112.f_ref
  2.3 1.6 reshape.113.g_ref
  3.9 1.6 reshape.114.a_ref
  5.5 37.2 %shard_map.110 = (bf16[4,128,512]{2,1,0:T(8,128)(2,1)}, bf16[4,128,512]{2,1,0:T(8,128)(2,1)}, bf16[4,128,512]{2,1,0:T(8,128)(2,1)}, bf16[3,512,128]{2,1,0:T(8,128)(2,1)}, bf16[128,512]{1,0:T(8,128)(2,1)}) custom-call(bf16[128,512]{1,0:T(8,128)(2,1)} %reshape.112.f_ref, bf16[128,512]{1,0:T(8,128)(2,1)} %reshape.113.g_ref, bf16[128,512]{1,0:T(8,128)(2,1)} %reshape.114.a_ref, ...), custom_call_target="tpu_custom_call" | custom-call | tf_op jit(solution)/shard_map/pallas_call | solution.py:219
  42.7 1.0 constant_dynamic-slice_fusion.3
  43.8 1.4 bitcast_reduce_fusion.1
  45.2 1.4 fusion.7
  47.2 0.7 fusion.37
  48.2 1.2 fusion.11
  49.6 15.4 %shard_map.111 = bf16[6,2,512,128]{3,2,1,0:T(8,128)(2,1)} custom-call(bf16[2,512,128]{2,1,0:T(8,128)(2,1)} %get-tuple-element.187.src_ref), custom_call_target="tpu_custom_call" | custom-call | tf_op jit(solution)/shard_map/pallas_call | solution.py:219
  65.0 2.8 %pad_maximum_fusion = bf16[7,2,512,128]{3,2,1,0:T(8,128)(2,1)} fusion(bf16[6,2,512,128]{3,2,1,0:T(8,128)(2,1)} %shard_map.111, bf16[1,2,512,128]{3,2,1,0:T(8,128)(2,1)S(1)} %get-tuple-element.186), kind=kLoop, calls=%fused_computation.20 | loop fusion | flops 917504 | bytes 3670016 | tf_op jit(solution)/shard_map/concatenate | solution.py:308
  67.8 2.7 %copy.15 = bf16[7,2,512,128]{2,3,1,0:T(8,128)(2,1)S(1)} copy(bf16[7,2,512,128]{3,2,1,0:T(8,128)(2,1)} %pad_maximum_fusion) | data formatting | bytes 3670016
  70.6 6.7 %while.26 = (s32[]{:T(128)}, f32[2,512]{1,0:T(2,128)S(1)}, f32[2,512]{1,0:T(2,128)S(1)}, bf16[7,2,512,128]{2,3,1,0:T(8,128)(2,1)S(1)}, bf16[512,2,64]{0,2,1:T(8,128)(2,1)S(1)}, /*index=5*/s32[]{:T(128)}, s32[]{:T(128)}) while((s32[]{:T(128)}, f32[2,512]{1,0:T(2,128)S(1)}, f32[2,512]{1,0:T(2,128)S(1)}, ...), condition=%wide.region_3.4_spmd.clone, body=%wide.region_0.0_spmd.clone.sunk | while | flops 69735424 | bytes 4771940 | solution.py:259
  70.6 0.5 bitcast_reduce_fusion.3
  71.6 0.5 bitcast_reduce_fusion.3
  72.6 0.5 bitcast_reduce_fusion.3
  73.5 0.5 bitcast_reduce_fusion.3
  74.5 0.5 bitcast_reduce_fusion.3
  75.4 0.5 bitcast_reduce_fusion.3
  76.4 0.5 bitcast_reduce_fusion.3
  77.3 22.7 %while.27 = (s32[]{:T(128)}, f32[512,2,64]{0,2,1:T(8,128)S(1)}, bf16[7,2,512,128]{3,2,1,0:T(8,128)(2,1)}, bf16[7,2,512,128]{2,3,1,0:T(8,128)(2,1)S(1)}, bf16[512...) while((s32[]{:T(128)}, f32[512,2,64]{0,2,1:T(8,128)S(1)}, ...), condition=%wide.region_6.7_spmd.clone, body=%wide.region_5.6_spmd.clone.sunk | while | flops 340131840 | bytes 10100887 | solution.py:277
  77.4 0.5 exponential_convert_fusion.2
  78.4 0.5 multiply_convert_fusion.2
  79.2 0.4 convolution_convert_fusion.13
  79.9 0.7 constant_dynamic-update-slice_fusion.2
  80.6 0.5 exponential_convert_fusion.2
  81.2 0.4 convolution_convert_fusion.12
  81.6 0.5 multiply_convert_fusion.2
  82.5 0.4 convolution_convert_fusion.13
  83.1 0.7 constant_dynamic-update-slice_fusion.2
  83.9 0.5 exponential_convert_fusion.2
  84.8 0.5 multiply_convert_fusion.2
  85.7 0.4 convolution_convert_fusion.13
  86.4 0.7 constant_dynamic-update-slice_fusion.2
  87.1 0.5 exponential_convert_fusion.2
  88.1 0.5 multiply_convert_fusion.2
  89.6 0.7 constant_dynamic-update-slice_fusion.2
  90.3 0.5 exponential_convert_fusion.2
  91.3 0.5 multiply_convert_fusion.2
  92.2 0.4 convolution_convert_fusion.13
  92.8 0.7 constant_dynamic-update-slice_fusion.2
  93.6 0.5 exponential_convert_fusion.2
  94.1 0.4 convolution_convert_fusion.12
  94.6 0.5 multiply_convert_fusion.2
  95.4 0.4 convolution_convert_fusion.13
  96.1 0.7 constant_dynamic-update-slice_fusion.2
  96.8 0.5 exponential_convert_fusion.2
  97.8 0.5 multiply_convert_fusion.2
  98.7 0.4 convolution_convert_fusion.13
  99.3 0.7 constant_dynamic-update-slice_fusion.2
  100.4 1.4 fusion.18
  101.8 1.2 slice.56.src_ref
  103.0 18.1 %shard_map.112 = bf16[6,2,512,128]{3,2,1,0:T(8,128)(2,1)} custom-call(bf16[6,2,512,128]{3,2,1,0:T(8,128)(2,1)} %slice.56.src_ref), custom_call_target="tpu_custom_call" | custom-call | tf_op jit(solution)/shard_map/pallas_call | solution.py:219
  121.2 1.7 %convert_reduce_fusion = f32[2,512,128]{2,1,0:T(8,128)S(1)} fusion(bf16[6,2,512,128]{3,2,1,0:T(8,128)(2,1)} %shard_map.112), kind=kLoop, calls=%fused_computation.19 | loop fusion | flops 1441792 | bytes 2097152 | tf_op jit(solution)/shard_map/reduce_sum | solution.py:312
  122.9 1.0 fusion.12
  124.2 1.1 fusion.5
  125.9 0.9 copy_bitcast_fusion.t_ref
  126.9 37.9 %shard_map.113 = (bf16[8,8,16,128]{3,2,1,0:T(8,128)(2,1)}, bf16[128,512]{1,0:T(8,128)(2,1)}) custom-call(bf16[4,8,64,128]{3,2,1,0:T(8,128)(2,1)} %copy_bitcast_fusion.t_ref, bf16[4,128,512]{2,1,0:T(8,128)(2,1)} %bitcast.188), custom_call_target="tpu_custom_call" | custom-call | tf_op jit(solution)/shard_map/pallas_call | solution.py:219
  164.8 1.6 reshape.125
  166.4 1.0 convert_bitcast_fusion
  167.5 0.7 copy.24
  168.1 0.7 copy.23
  168.8 0.7 copy.22
  169.5 0.7 copy.21
  (95 shorter events, 11.6 us)
Async XLA Ops:
  42.7 4.0 %copy-start = (bf16[4,128,512]{2,1,0:T(8,128)(2,1)S(1)}, bf16[4,128,512]{2,1,0:T(8,128)(2,1)}, u32[]{:S(2)}) copy-start(bf16[4,128,512]{2,1,0:T(8,128)(2,1)} %get-tuple-element.83) | copy-start | bytes 1572868
  42.7 4.0 %copy-start.2 = (bf16[3,512,128]{2,1,0:T(8,128)(2,1)S(1)}, bf16[3,512,128]{2,1,0:T(8,128)(2,1)}, u32[]{:S(2)}) copy-start(bf16[3,512,128]{2,1,0:T(8,128)(2,1)} %get-tuple-element.84) | copy-start | bytes 1179652
  43.8 4.2 %copy-start.4 = (bf16[4,128,512]{2,1,0:T(8,128)(2,1)S(1)}, bf16[4,128,512]{2,1,0:T(8,128)(2,1)}, u32[]{:S(2)}) copy-start(bf16[4,128,512]{2,1,0:T(8,128)(2,1)} %get-tuple-element.89) | copy-start | bytes 1572868
  100.0 1.7 %copy-start.1 = (bf16[7,2,512,128]{3,2,1,0:T(8,128)(2,1)S(1)}, bf16[7,2,512,128]{3,2,1,0:T(8,128)(2,1)}, u32[]{:S(2)}) copy-start(bf16[7,2,512,128]{3,2,1,0:T(8,128)(2,1)} %get-tuple-element.91) | copy-start | bytes 5505028
  121.2 2.8 %copy-start.3 = (bf16[3,512,128]{2,1,0:T(8,128)(2,1)S(1)}, bf16[3,512,128]{2,1,0:T(8,128)(2,1)}, u32[]{:S(2)}) copy-start(bf16[3,512,128]{2,1,0:T(8,128)(2,1)} %get-tuple-element.84) | copy-start | bytes 1179652

commit v2 on v1

--- a/solution.py
+++ b/solution.py
@@ -1,6 +1,3 @@
-import functools
-import math
-
 import jax
 import jax.numpy as jnp
 from jax import lax
@@ -111,17 +108,114 @@
         onward[i].wait()
 
 
-def swap_kernel(sign, src_ref, dst_ref, send, recv):
+def attend_kernel(
+    q_ref, g_ref, delta_ref, own_ref, dq_ref, dkv_ref,
+    kv, scores, part, back, qt, gt, kt, qs, gs, prob, grad, dqt, top, total,
+    ksend, krecv, bsend, brecv,
+):
     index = {axis: lax.axis_index(axis) for axis in ("gx", "gy", "gz")}
+    tokens, width = q_ref.shape
+    chunk = tokens // 2
     greet([ring(axis, index[axis], step) for axis, step in STEPS])
-    copies = []
-    for k in (4, 5, 0, 1, 2, 3):
+
+    def outward(i, k):
         axis, step = STEPS[k]
-        src = src_ref.at[k] if sign < 0 else src_ref
-        copies.append(remote(src, dst_ref.at[k], send.at[k], recv.at[k], ring(axis, index[axis], sign * step)))
-        copies[-1].start()
-    for copy in copies:
-        copy.wait()
+        return remote(own_ref.at[i], kv.at[k + 1, i], ksend.at[i, k + 1], krecv.at[i, k + 1], ring(axis, index[axis], step))
+
+    def homeward(slot):
+        pair = lax.div(slot - 1, 2)
+        sign = 1 - 2 * lax.rem(slot - 1, 2)
+        at_z = lax.div(pair, 2)
+        at_y = pair - 2 * at_z
+        at_x = 1 - at_y - at_z
+        device = {
+            "gx": lax.rem(index["gx"] - at_x * sign + 8, 8),
+            "gy": lax.rem(index["gy"] - 2 * at_y * sign + 8, 8),
+            "gz": lax.rem(index["gz"] - 2 * at_z * sign + 8, 8),
+        }
+        return remote(part.at[slot], back.at[slot], bsend.at[slot], brecv.at[slot], device)
+
+    for i in range(2):
+        for k in (4, 5, 0, 1, 2, 3):
+            outward(i, k).start()
+
+    kv[0] = own_ref[...]
+    scaled = q_ref[...].astype(F32) * 0.125
+    upstream = g_ref[...].astype(F32)
+    row_head = lax.broadcasted_iota(jnp.int32, (width, tokens), 0) // (width // 2)
+    lane_head = lax.broadcasted_iota(jnp.int32, (tokens, width), 1) // (width // 2)
+    for value, turned, stacked in ((scaled, qt, qs), (upstream, gt, gs)):
+        flipped = value.T
+        for head in range(2):
+            turned[:, head * tokens : (head + 1) * tokens] = jnp.where(row_head == head, flipped, 0.0).astype(BF16)
+            stacked[head * tokens : (head + 1) * tokens, :] = jnp.where(lane_head == head, value, 0.0).astype(BF16)
+    top[...] = jnp.full_like(top, -jnp.inf)
+    total[...] = jnp.zeros_like(total)
+    dqt[...] = jnp.zeros_like(dqt)
+
+    def arrived(i, slot):
+        return remote(own_ref.at[i], kv.at[slot, i], ksend.at[i, slot], krecv.at[i, slot], ring("gx", index["gx"], 1))
+
+    def first_pass(slot, unused):
+        @pl.when(slot > 0)
+        def _():
+            arrived(0, slot).wait_recv()
+
+        for c in range(4):
+            columns = slice(c * chunk, (c + 1) * chunk)
+            block = dot(kv[slot, 0], qt[:, columns])
+            scores[slot, :, columns] = block
+            old_top = top[:, columns]
+            new_top = jnp.maximum(old_top, jnp.max(block, axis=0, keepdims=True))
+            summed = jnp.sum(jnp.exp(block - new_top), axis=0, keepdims=True)
+            total[:, columns] = total[:, columns] * jnp.exp(old_top - new_top) + summed
+            top[:, columns] = new_top
+        return unused
+
+    lax.fori_loop(0, 7, first_pass, 0)
+    top[...] = top[...] + jnp.log(total[...])
+
+    def second_pass(turn, unused):
+        last = lax.div(turn, 6)
+        group = lax.div(turn, 2)
+        slot = (1 + 2 * (2 * group - 3 * lax.div(group, 2)) + lax.rem(turn, 2)) * (1 - last)
+
+        @pl.when(turn < 6)
+        def _():
+            arrived(1, slot).wait_recv()
+
+        kt[...] = kv[slot, 0].astype(F32).T.astype(BF16)
+        for c in range(4):
+            columns = slice(c * chunk, (c + 1) * chunk)
+            p = jnp.exp(scores[slot, :, columns] - top[:, columns]).astype(BF16)
+            prob[:, columns] = p
+            dp = dot(kv[slot, 1], gt[:, columns])
+            ds = (p.astype(F32) * (dp - delta_ref[:, columns])).astype(BF16)
+            grad[:, columns] = ds
+            dqt[:, columns] += dot(kt[...], ds)
+        part[slot, 0] = dot(grad[...], qs[...]).astype(BF16)
+        part[slot, 1] = dot(prob[...], gs[...]).astype(BF16)
+
+        @pl.when(turn < 6)
+        def _():
+            homeward(slot).start()
+
+        return unused
+
+    lax.fori_loop(0, 7, second_pass, 0)
+    half = width // 2
+    turned = jnp.concatenate([dqt[:half, :tokens], dqt[half:, tokens:]], axis=0) * 0.125
+    dq_ref[...] = turned.T.astype(BF16)
+    for i in range(2):
+        for k in range(6):
+            outward(i, k).wait_send()
+    for slot in (1, 2, 5, 6, 3, 4):
+        homeward(slot).wait()
+    for i in range(2):
+        whole = part[0, i].astype(F32)
+        for slot in range(1, 7):
+            whole = whole + back[slot, i].astype(F32)
+        dkv_ref[i] = whole.astype(BF16)
 
 
 def reduce_kernel(
@@ -238,46 +332,6 @@
     return jnp.dot(left, right, preferred_element_type=F32)
 
 
-def attention(query, grad, row_delta, nearby):
-    tokens, quarter = query.shape
-    head_dim = 64
-    group_heads = quarter // head_dim
-    score_scale = 1.0 / math.sqrt(head_dim)
-    query_heads = query.reshape(tokens, group_heads, head_dim)
-    grad_heads = grad.reshape(tokens, group_heads, head_dim)
-
-    def first_pass(carry, key_value):
-        row_top, row_total = carry
-        key_heads = key_value[0].reshape(tokens, group_heads, head_dim)
-        scores = jnp.einsum("qhd,khd->hqk", query_heads, key_heads, preferred_element_type=F32) * score_scale
-        new_top = jnp.maximum(row_top, jnp.max(scores, axis=2))
-        row_total = row_total * jnp.exp(row_top - new_top) + jnp.sum(jnp.exp(scores - new_top[:, :, None]), axis=2)
-        return ((new_top, row_total), None)
-
-    start_top = jnp.full((group_heads, tokens), -jnp.inf, F32)
-    start_total = jnp.zeros((group_heads, tokens), F32)
-    stats, unused = lax.scan(first_pass, (start_top, start_total), nearby)
-    log_total = stats[0] + jnp.log(stats[1])
-
-    def second_pass(query_grad, key_value):
-        key_heads = key_value[0].reshape(tokens, group_heads, head_dim)
-        value_heads = key_value[1].reshape(tokens, group_heads, head_dim)
-        scores = jnp.einsum("qhd,khd->hqk", query_heads, key_heads, preferred_element_type=F32) * score_scale
-        prob = jnp.exp(scores - log_total[:, :, None]).astype(BF16)
-        prob_grad = jnp.einsum("qhd,khd->hqk", grad_heads, value_heads, preferred_element_type=F32)
-        score_grad = (prob.astype(F32) * (prob_grad - row_delta[:, :, None]) * score_scale).astype(BF16)
-        query_grad = query_grad + jnp.einsum("hqk,khd->qhd", score_grad, key_heads, preferred_element_type=F32)
-        key_grad = jnp.einsum("hqk,qhd->khd", score_grad, query_heads, preferred_element_type=F32)
-        value_grad = jnp.einsum("hqk,qhd->khd", prob, grad_heads, preferred_element_type=F32)
-        key_grad = key_grad.astype(BF16).reshape(tokens, quarter)
-        value_grad = value_grad.astype(BF16).reshape(tokens, quarter)
-        return (query_grad, jnp.stack([key_grad, value_grad]))
-
-    start_grad = jnp.zeros((tokens, group_heads, head_dim), F32)
-    query_grad, partials = lax.scan(second_pass, start_grad, nearby)
-    return query_grad.reshape(tokens, quarter).astype(BF16), partials
-
-
 def on_device(features, grad_y, attn_out, w_query, w_key, w_value, w_out):
     width = features.shape[3]
     local = features.shape[0] * features.shape[1] * features.shape[2]
@@ -300,16 +354,31 @@
     query, key, value = (dot(fb, w3[i]).astype(BF16) for i in range(3))
     grad = transpose_dot(gb, wo).astype(BF16)
     own_pair = jnp.stack([key, value])
-    (near,) = call(
-        functools.partial(swap_kernel, 1), 1, [(6, 2, tokens, quarter)], [dma(6), dma(6)], own_pair
-    )
     products = grad.astype(F32) * own_ab.astype(F32)
-    row_delta = jnp.sum(products.reshape(tokens, 2, quarter // 2), axis=2).T
-    query_grad, partials = attention(query, grad, row_delta, jnp.concatenate([own_pair[None], near]))
-    (back,) = call(
-        functools.partial(swap_kernel, -1), 2, [(6, 2, tokens, quarter)], [dma(6), dma(6)], partials[1:]
-    )
-    pair_grads = (partials[0].astype(F32) + jnp.sum(back.astype(F32), axis=0)).astype(BF16)
+    row_delta = jnp.sum(products.reshape(tokens, 2, quarter // 2), axis=2).T.reshape(1, 2 * tokens)
+    query_grad, pair_grads = call(
+        attend_kernel,
+        1,
+        [(tokens, quarter), (2, tokens, quarter)],
+        [
+            pltpu.VMEM((7, 2, tokens, quarter), BF16),
+            pltpu.VMEM((7, tokens, 2 * tokens), F32),
+            pltpu.VMEM((7, 2, tokens, quarter), BF16),
+            pltpu.VMEM((7, 2, tokens, quarter), BF16),
+            pltpu.VMEM((quarter, 2 * tokens), BF16),
+            pltpu.VMEM((quarter, 2 * tokens), BF16),
+            pltpu.VMEM((quarter, tokens), BF16),
+            pltpu.VMEM((2 * tokens, quarter), BF16),
+            pltpu.VMEM((2 * tokens, quarter), BF16),
+            pltpu.VMEM((tokens, 2 * tokens), BF16),
+            pltpu.VMEM((tokens, 2 * tokens), BF16),
+            pltpu.VMEM((quarter, 2 * tokens), F32),
+            pltpu.VMEM((1, 2 * tokens), F32),
+            pltpu.VMEM((1, 2 * tokens), F32),
+            dma(2, 7), dma(2, 7), dma(7), dma(7),
+        ],
+        query, grad, row_delta, own_pair,
+    )
     grads = (query_grad, pair_grads[0], pair_grads[1])
     partial_x = sum(transpose_dot(grads[i], w3[i]) for i in range(3))
     partial_x = partial_x.astype(BF16).reshape(4, local, width)
@@ -318,7 +387,7 @@
     terms = terms.reshape(4, 8, 64, quarter)
     rows, grad_x = call(
         reduce_kernel,
-        3,
+        2,
         [(8, 8, 16, quarter), (local, width)],
         [
             pltpu.VMEM((3, 8, 64, quarter), BF16),

time: 171 us -> 129 us (0.75)
  matrix products: 27.6 us -> 7.45 us
  local copies, waits for them, and re-layouts: 21.1 us -> 10.3 us
  other arithmetic: 11.2 us -> 1.76 us
    dot_general x42 -> x0, matrix products: 19.3 us -> none  [the longest x7 3.79 us: second_pass(): jnp.einsum('qhd,khd->hqk', query_heads, key_heads, preferred_element_type...]
    dynamic_update_slice x14 -> x0, local copies, waits for them, and re-layouts: 6.24 us -> none  [attention(): query_grad, partials = lax.scan(second_pass, start_grad, nearby)]
    reduce_sum x8 -> x1, other arithmetic: 4.27 us -> 0.03 us  [on_device(): jnp.sum(products.reshape(tokens, 2, quarter // 2), axis=2)]
    concatenate x1 -> x0, other arithmetic: 2.83 us -> none  [on_device(): jnp.concatenate([own_pair[None], near])]
    pallas_call x4 -> x3, Pallas kernels: 109 us -> 108 us  [call(): pl.pallas_call(kernel, out_shape=[jax.ShapeDtypeStruct(shape, BF16) for s...]
where the time goes in v2:
time: 129 us; the launch traced here: 128 us
  Pallas kernels  108 us (84%)
  local copies, waits for them, and re-layouts  10.3 us (8%)
  matrix products  7.45 us (6%)
  other arithmetic  1.76 us (1%)
    pallas_call x3, Pallas kernels, call(): pl.pallas_call(kernel, out_shape=[jax.ShapeDtypeStruct(shape, BF16) for s...  108 us
    dot_general x3, matrix products, dot(): return jnp.dot(left, right, preferred_element_type=F32)  3.61 us
    slice x5, local copies, waits for them, and re-layouts, on_device(): return (grad_x.reshape(features.shape), rows[0], rows[1], rows[2], rows[3])  2.69 us
    dot_general x4, matrix products, transpose_dot(): lax.dot_general(left, right, (((1,), (1,)), ((), ())), preferred_element_...  2.64 us

profile of v2, /device:TPU:1, one launch (start us, length us, event | category | flops | bytes accessed | tf_op | source)
XLA Modules:
  0.0 128.2 jit_solution(1122520671908611275)
XLA Ops:
  0.7 0.0 copy-start.8
  0.7 1.6 %reshape.89.f_ref = bf16[128,512]{1,0:T(8,128)(2,1)} reshape(bf16[8,4,4,512]{3,2,1,0:T(4,128)(2,1)} %param.7) | data formatting | bytes 262144 | tf_op jit(solution)/shard_map/reshape | solution.py:340
  2.3 0.0 copy-done.8
  2.3 0.0 copy-start.9
  2.3 0.7 reshape.90.g_ref
  3.0 0.2 copy-done.9
  3.2 0.7 reshape.91.a_ref
  3.9 37.2 %shard_map.110 = (bf16[4,128,512]{2,1,0:T(8,128)(2,1)}, bf16[4,128,512]{2,1,0:T(8,128)(2,1)}, bf16[4,128,512]{2,1,0:T(8,128)(2,1)}, bf16[3,512,128]{2,1,0:T(8,128)(2,1)}, bf16[128,512]{1,0:T(8,128)(2,1)}) custom-call(bf16[128,512]{1,0:T(8,128)(2,1)} %reshape.89.f_ref, bf16[128,512]{1,0:T(8,128)(2,1)} %reshape.90.g_ref, bf16[128,512]{1,0:T(8,128)(2,1)} %reshape.91.a_ref, ...), custom_call_target="tpu_custom_call" | custom-call | tf_op jit(solution)/shard_map/pallas_call | solution.py:313
  41.1 0.0 copy-start
  41.1 1.4 %fusion.1 = bf16[1,512,128]{2,1,0:T(8,128)(2,1)S(1)} fusion(bf16[512,512]{1,0:T(8,128)(2,1)} %bitcast.94, bf16[3,512,128]{2,1,0:T(8,128)(2,1)} %get-tuple-element.15), kind=kOutput, calls=%fused_computation.11 | convolution fusion | flops 67174400 | bytes 786432 | tf_op jit(solution)/shard_map/dot_general | solution.py:332
  42.6 0.0 copy-done
  42.6 0.0 copy-start.1
  42.6 1.9 %convolution_convert_fusion.7.q_ref = bf16[512,128]{1,0:T(8,128)(2,1)} fusion(bf16[512,512]{1,0:T(8,128)(2,1)S(1)} %bitcast.95, bf16[3,512,128]{2,1,0:T(8,128)(2,1)} %get-tuple-element.15), kind=kOutput, calls=%fused_computation.10 | convolution fusion | flops 67174400 | bytes 786432 | tf_op jit(solution)/shard_map/dot_general | solution.py:332
  44.5 0.0 copy-done.1
  44.5 0.0 copy-start.3
  44.5 0.0 copy-start.4
  44.5 0.3 fusion.2
  44.8 0.0 copy-start.7
  44.8 0.7 pad_maximum_fusion.own_ref
  45.5 0.0 copy-done.3
  45.5 0.1 copy-done.4
  45.7 0.1 copy-done.7
  45.8 1.0 convert_multiply_fusion
  46.7 0.1 copy.22
  46.9 0.6 copy.34
  47.5 36.6 %shard_map.111 = (bf16[512,128]{1,0:T(8,128)(2,1)}, bf16[2,512,128]{2,1,0:T(8,128)(2,1)}) custom-call(bf16[512,128]{1,0:T(8,128)(2,1)} %convolution_convert_fusion.7.q_ref, bf16[512,128]{1,0:T(8,128)(2,1)} %get-tuple-element.28.g_ref, f32[1,1024]{1,0:T(1,128)} %bitcast.112, bf16[2,512,128]{2,1,0:T(8,128)(2,1)} %pad_maximum_fusion.own_ref), custom_call_target="tpu_custom_call" | custom-call | tf_op jit(solution)/shard_map/pallas_call | solution.py:313
  84.1 0.2 copy.23
  84.3 0.3 fusion.6
  84.6 0.0 copy-start.2
  84.7 0.2 copy.20
  84.9 0.7 copy-done.2
  85.6 0.3 fusion.5
  85.9 0.0 copy-start.5
  85.9 0.3 fusion.4
  86.2 0.6 copy-done.5
  86.8 0.3 fusion.3
  87.1 0.9 copy_bitcast_fusion.t_ref
  88.0 0.3 fusion.17
  88.3 0.3 convolution_add_fusion.1
  88.7 1.1 fusion
  89.7 34.1 %shard_map.112 = (bf16[8,8,16,128]{3,2,1,0:T(8,128)(2,1)}, bf16[128,512]{1,0:T(8,128)(2,1)}) custom-call(bf16[4,8,64,128]{3,2,1,0:T(8,128)(2,1)} %copy_bitcast_fusion.t_ref, bf16[4,128,512]{2,1,0:T(8,128)(2,1)} %bitcast.101), custom_call_target="tpu_custom_call" | custom-call | tf_op jit(solution)/shard_map/pallas_call | solution.py:313
  123.8 0.0 copy-start.6
  123.8 1.6 %reshape.101 = bf16[8,4,4,512]{3,2,1,0:T(4,128)(2,1)} reshape(bf16[128,512]{1,0:T(8,128)(2,1)} %get-tuple-element.21) | data formatting | bytes 262144 | tf_op jit(solution)/shard_map/reshape | solution.py:405
  125.5 0.0 copy-done.6
  125.6 0.7 copy.28
  126.2 0.7 copy.27
  126.9 0.7 copy.26
  127.6 0.7 copy.25
  (3 shorter events, 0.1 us)
Async XLA Ops:
  0.7 1.6 %copy-start.8 = (bf16[8,4,4,512]{3,2,1,0:T(4,128)(2,1)S(1)}, bf16[8,4,4,512]{3,2,1,0:T(4,128)(2,1)}, u32[]{:S(2)}) copy-start(bf16[8,4,4,512]{3,2,1,0:T(4,128)(2,1)} %param.8) | copy-start | bytes 393220
  2.3 0.9 copy-start.9
  41.1 1.4 %copy-start = (bf16[4,128,512]{2,1,0:T(8,128)(2,1)S(1)}, bf16[4,128,512]{2,1,0:T(8,128)(2,1)}, u32[]{:S(2)}) copy-start(bf16[4,128,512]{2,1,0:T(8,128)(2,1)} %get-tuple-element.14) | copy-start | bytes 1572868
  42.6 1.9 %copy-start.1 = (bf16[3,512,128]{2,1,0:T(8,128)(2,1)S(1)}, bf16[3,512,128]{2,1,0:T(8,128)(2,1)}, u32[]{:S(2)}) copy-start(bf16[3,512,128]{2,1,0:T(8,128)(2,1)} %get-tuple-element.15) | copy-start | bytes 1179652
  44.5 1.1 copy-start.3
  44.5 1.2 copy-start.4
  44.8 1.0 copy-start.7
  84.6 1.0 copy-start.2
  85.9 0.9 copy-start.5
  123.8 1.6 %copy-start.6 = (bf16[8,8,16,128]{3,2,1,0:T(8,128)(2,1)S(1)}, bf16[8,8,16,128]{3,2,1,0:T(8,128)(2,1)}, u32[]{:S(2)}) copy-start(bf16[8,8,16,128]{3,2,1,0:T(8,128)(2,1)} %get-tuple-element.22) | copy-start | bytes 786436

commit v3 on v2

--- a/solution.py
+++ b/solution.py
@@ -29,37 +29,51 @@
     return {axis: lax.rem(index + step + 8, 8)}
 
 
-def gather_kernel(
+def block_kernel(
     f_ref, g_ref, a_ref, wq_ref, wk_ref, wv_ref, wo_ref,
-    fb_ref, gb_ref, ab_ref, w3_ref, wob_ref,
-    bsend, brecv, wsend, wrecv, osend, orecv,
+    fb_ref, ab_ref, gown_ref, w3_ref, dq_ref, dkv_ref,
+    gb_ref, wob_ref, own_ref, delta_ref,
+    kv, scores, part, back, qt, gt, kt, qs, gs, prob, grad, dqt, top, total,
+    rsend, rrecv, wsend, wrecv, osend, orecv,
+    ksend, krecv, bsend, brecv,
 ):
-    gy, gz = lax.axis_index("gy"), lax.axis_index("gz")
+    index = {axis: lax.axis_index(axis) for axis in ("gx", "gy", "gz")}
+    gy, gz = index["gy"], index["gz"]
+    tokens, width = dq_ref.shape
+    local = f_ref.shape[0]
+    chunk = tokens // 2
     y_bit, z_bit = lax.rem(gy, 2), lax.rem(gz, 2)
     pair_z = {"gz": gz + 1 - 2 * z_bit}
     pair_y = {"gy": gy + 1 - 2 * y_bit}
-    slot = 2 * y_bit + z_bit
-    slot_y = 2 * (1 - y_bit) + z_bit
-    greet([ring("gz", gz, d) for d in range(1, 8)] + [pair_y])
+    own_columns = pl.ds(pl.multiple_of(z_bit * 256 + y_bit * 128, 128), 128)
+    greet(
+        [ring("gz", gz, d) for d in range(1, 8)]
+        + [pair_y]
+        + [ring(axis, index[axis], step) for axis, step in STEPS[:4]]
+    )
+
+    def slot_rows(slot):
+        return pl.ds(pl.multiple_of(slot * local, local), local)
+
+    mine = slot_rows(2 * y_bit + z_bit)
+    theirs = slot_rows(2 * (1 - y_bit) + z_bit)
     trios = ((f_ref, fb_ref), (g_ref, gb_ref), (a_ref, ab_ref))
-    to_y, to_z, onward = [], [], []
-    for i, (src, dst) in enumerate(trios):
-        to_y.append(remote(src, dst.at[slot], bsend.at[0, i], brecv.at[0, i], pair_y))
-        to_z.append(remote(src, dst.at[slot], bsend.at[1, i], brecv.at[1, i], pair_z))
-        to_y[-1].start()
-        to_z[-1].start()
+    to_y = [remote(src, dst.at[mine], rsend.at[0, i], rrecv.at[0, i], pair_y) for i, (src, dst) in enumerate(trios)]
+    to_z = [remote(src, dst.at[mine], rsend.at[1, i], rrecv.at[1, i], pair_z) for i, (src, dst) in enumerate(trios)]
+    onward = [
+        remote(dst.at[theirs], dst.at[theirs], rsend.at[2, i], rrecv.at[2, i], pair_z)
+        for i, (src, dst) in enumerate(trios)
+    ]
     weights = (wq_ref, wk_ref, wv_ref)
-    rows = pl.ds(pl.multiple_of(gz * 64, 64), 64)
-    weight_copies = []
-    for d in (4, 3, 5, 2, 6, 1, 7):
+    weight_rows = pl.ds(pl.multiple_of(gz * 64, 64), 64)
+
+    def weight_copy(i, d):
         target = lax.rem(gz + d, 8)
         columns = pl.ds(pl.multiple_of(lax.rem(target, 2) * 256 + y_bit * 128, 128), 128)
-        for i, w_ref in enumerate(weights):
-            copy = remote(
-                w_ref.at[:, columns], w3_ref.at[i, rows], wsend.at[d - 1, i], wrecv.at[d - 1, i], {"gz": target}
-            )
-            copy.start()
-            weight_copies.append(copy)
+        return remote(
+            weights[i].at[:, columns], w3_ref.at[i, weight_rows], wsend.at[d - 1, i], wrecv.at[d - 1, i], {"gz": target}
+        )
+
     half = lax.rem(gz, 2)
     out_core = lax.div(gz, 4)
     out_from = lax.rem(lax.div(gz, 2), 2) == y_bit
@@ -68,55 +82,34 @@
     def out_copy(zh):
         return remote(wo_ref, wob_ref.at[out_rows], osend.at[zh], orecv.at[half], {"gz": 2 * zh + out_core})
 
-    for zh in range(4):
-
-        @pl.when(jnp.logical_and(out_from, 2 * zh + out_core != gz))
-        def _():
-            out_copy(zh).start()
-
-    columns = pl.ds(pl.multiple_of(z_bit * 256 + y_bit * 128, 128), 128)
-    for i, w_ref in enumerate(weights):
-        w3_ref[i, rows] = w_ref[:, columns]
-    for src, dst in trios:
-        dst[slot] = src[...]
-    for i, (src, dst) in enumerate(trios):
+    def begin_share(i):
+        to_y[i].start()
+        to_z[i].start()
+        src, dst = trios[i]
+        dst[mine] = src[...]
+
+    def pass_on(i):
         to_y[i].wait_recv()
-        onward.append(remote(dst.at[slot_y], dst.at[slot_y], bsend.at[2, i], brecv.at[2, i], pair_z))
-        onward[-1].start()
-    for s in range(2):
-        source = 4 * z_bit + 2 * y_bit + s
-
-        @pl.when(source != gz)
-        def _():
-            remote(wo_ref, wob_ref.at[pl.ds(s * 64, 64)], osend.at[0], orecv.at[s], {"gz": source}).wait_recv()
-
-        @pl.when(source == gz)
-        def _():
-            wob_ref[pl.ds(s * 64, 64)] = wo_ref[...]
-
-    for copy in weight_copies:
-        copy.wait()
-    for zh in range(4):
-
-        @pl.when(jnp.logical_and(out_from, 2 * zh + out_core != gz))
-        def _():
-            out_copy(zh).wait_send()
-
-    for i in range(3):
-        to_y[i].wait_send()
-        to_z[i].wait()
-        onward[i].wait()
-
-
-def attend_kernel(
-    q_ref, g_ref, delta_ref, own_ref, dq_ref, dkv_ref,
-    kv, scores, part, back, qt, gt, kt, qs, gs, prob, grad, dqt, top, total,
-    ksend, krecv, bsend, brecv,
-):
-    index = {axis: lax.axis_index(axis) for axis in ("gx", "gy", "gz")}
-    tokens, width = q_ref.shape
-    chunk = tokens // 2
-    greet([ring(axis, index[axis], step) for axis, step in STEPS])
+        onward[i].start()
+
+    def end_share(i):
+        to_z[i].wait_recv()
+        onward[i].wait_recv()
+
+    order = (4, 3, 5, 2, 6, 1, 7)
+    begin_share(0)
+    for i in (1, 0, 2):
+        for d in order:
+            weight_copy(i, d).start()
+        w3_ref[i, weight_rows] = weights[i][:, own_columns]
+    begin_share(1)
+    pass_on(0)
+    end_share(0)
+
+    def project(i):
+        for d in order:
+            weight_copy(i, d).wait_recv()
+        return dot(fb_ref[...], w3_ref[i])
 
     def outward(i, k):
         axis, step = STEPS[k]
@@ -135,23 +128,37 @@
         }
         return remote(part.at[slot], back.at[slot], bsend.at[slot], brecv.at[slot], device)
 
-    for i in range(2):
-        for k in (4, 5, 0, 1, 2, 3):
-            outward(i, k).start()
-
-    kv[0] = own_ref[...]
-    scaled = q_ref[...].astype(F32) * 0.125
-    upstream = g_ref[...].astype(F32)
     row_head = lax.broadcasted_iota(jnp.int32, (width, tokens), 0) // (width // 2)
     lane_head = lax.broadcasted_iota(jnp.int32, (tokens, width), 1) // (width // 2)
-    for value, turned, stacked in ((scaled, qt, qs), (upstream, gt, gs)):
+
+    def spread(value, turned, stacked):
         flipped = value.T
         for head in range(2):
             turned[:, head * tokens : (head + 1) * tokens] = jnp.where(row_head == head, flipped, 0.0).astype(BF16)
             stacked[head * tokens : (head + 1) * tokens, :] = jnp.where(lane_head == head, value, 0.0).astype(BF16)
+
+    def send_own(i, w):
+        value = project(w).astype(BF16)
+        own_ref[i] = value
+        kv[0, i] = value
+        for k in (4, 5, 0, 1, 2, 3):
+            outward(i, k).start()
+
+    send_own(0, 1)
+    for zh in range(4):
+
+        @pl.when(jnp.logical_and(out_from, 2 * zh + out_core != gz))
+        def _():
+            out_copy(zh).start()
+
+    begin_share(2)
+    send_own(1, 2)
+    pass_on(1)
+    spread(project(0).astype(BF16).astype(F32) * 0.125, qt, qs)
     top[...] = jnp.full_like(top, -jnp.inf)
     total[...] = jnp.zeros_like(total)
     dqt[...] = jnp.zeros_like(dqt)
+    pass_on(2)
 
     def arrived(i, slot):
         return remote(own_ref.at[i], kv.at[slot, i], ksend.at[i, slot], krecv.at[i, slot], ring("gx", index["gx"], 1))
@@ -174,6 +181,26 @@
 
     lax.fori_loop(0, 7, first_pass, 0)
     top[...] = top[...] + jnp.log(total[...])
+    for s in range(2):
+        source = 4 * z_bit + 2 * y_bit + s
+
+        @pl.when(source != gz)
+        def _():
+            remote(wo_ref, wob_ref.at[pl.ds(s * 64, 64)], osend.at[0], orecv.at[s], {"gz": source}).wait_recv()
+
+        @pl.when(source == gz)
+        def _():
+            wob_ref[pl.ds(s * 64, 64)] = wo_ref[...]
+
+    end_share(1)
+    end_share(2)
+    gown_ref[...] = gb_ref[:, own_columns]
+    upstream = transpose_dot(gb_ref[...], wob_ref[...]).astype(BF16).astype(F32)
+    spread(upstream, gt, gs)
+    products = (upstream * ab_ref[:, own_columns].astype(F32)).T
+    for head in range(2):
+        rows = products[head * (width // 2) : (head + 1) * (width // 2)]
+        delta_ref[:, head * tokens : (head + 1) * tokens] = jnp.sum(rows, axis=0, keepdims=True)
 
     def second_pass(turn, unused):
         last = lax.div(turn, 6)
@@ -203,9 +230,21 @@
         return unused
 
     lax.fori_loop(0, 7, second_pass, 0)
-    half = width // 2
-    turned = jnp.concatenate([dqt[:half, :tokens], dqt[half:, tokens:]], axis=0) * 0.125
+    middle = width // 2
+    turned = jnp.concatenate([dqt[:middle, :tokens], dqt[middle:, tokens:]], axis=0) * 0.125
     dq_ref[...] = turned.T.astype(BF16)
+    for i in range(3):
+        to_y[i].wait_send()
+        to_z[i].wait_send()
+        onward[i].wait_send()
+        for d in order:
+            weight_copy(i, d).wait_send()
+    for zh in range(4):
+
+        @pl.when(jnp.logical_and(out_from, 2 * zh + out_core != gz))
+        def _():
+            out_copy(zh).wait_send()
+
     for i in range(2):
         for k in range(6):
             outward(i, k).wait_send()
@@ -340,27 +379,15 @@
     feature_rows = features.reshape(local, width)
     dy_rows = grad_y.reshape(local, width)
     saved_rows = attn_out.reshape(local, width)
-    fb, gb, ab, w3, wo = call(
-        gather_kernel,
+    fb, ab, own_gb, w3, query_grad, pair_grads = call(
+        block_kernel,
         0,
-        [(4, local, width)] * 3 + [(3, width, quarter), (quarter, width)],
-        [dma(3, 3), dma(3, 3), dma(7, 3), dma(7, 3), dma(4), dma(2)],
-        feature_rows, dy_rows, saved_rows, w_query, w_key, w_value, w_out,
-    )
-    fb, gb, ab = (block.reshape(tokens, width) for block in (fb, gb, ab))
-    start = (lax.axis_index("gz") % 2) * (2 * quarter) + (lax.axis_index("gy") % 2) * quarter
-    own_gb = lax.dynamic_slice_in_dim(gb, start, quarter, 1)
-    own_ab = lax.dynamic_slice_in_dim(ab, start, quarter, 1)
-    query, key, value = (dot(fb, w3[i]).astype(BF16) for i in range(3))
-    grad = transpose_dot(gb, wo).astype(BF16)
-    own_pair = jnp.stack([key, value])
-    products = grad.astype(F32) * own_ab.astype(F32)
-    row_delta = jnp.sum(products.reshape(tokens, 2, quarter // 2), axis=2).T.reshape(1, 2 * tokens)
-    query_grad, pair_grads = call(
-        attend_kernel,
-        1,
-        [(tokens, quarter), (2, tokens, quarter)],
+        [(tokens, width), (tokens, width), (tokens, quarter), (3, width, quarter), (tokens, quarter), (2, tokens, quarter)],
         [
+            pltpu.VMEM((tokens, width), BF16),
+            pltpu.VMEM((quarter, width), BF16),
+            pltpu.VMEM((2, tokens, quarter), BF16),
+            pltpu.VMEM((1, 2 * tokens), F32),
             pltpu.VMEM((7, 2, tokens, quarter), BF16),
             pltpu.VMEM((7, tokens, 2 * tokens), F32),
             pltpu.VMEM((7, 2, tokens, quarter), BF16),
@@ -375,9 +402,10 @@
             pltpu.VMEM((quarter, 2 * tokens), F32),
             pltpu.VMEM((1, 2 * tokens), F32),
             pltpu.VMEM((1, 2 * tokens), F32),
+            dma(3, 3), dma(3, 3), dma(7, 3), dma(7, 3), dma(4), dma(2),
             dma(2, 7), dma(2, 7), dma(7), dma(7),
         ],
-        query, grad, row_delta, own_pair,
+        feature_rows, dy_rows, saved_rows, w_query, w_key, w_value, w_out,
     )
     grads = (query_grad, pair_grads[0], pair_grads[1])
     partial_x = sum(transpose_dot(grads[i], w3[i]) for i in range(3))
@@ -387,7 +415,7 @@
     terms = terms.reshape(4, 8, 64, quarter)
     rows, grad_x = call(
         reduce_kernel,
-        2,
+        1,
         [(8, 8, 16, quarter), (local, width)],
         [
             pltpu.VMEM((3, 8, 64, quarter), BF16),

time: 129 us -> 122 us (0.946)
  matrix products: 7.45 us -> 4.08 us
  local copies, waits for them, and re-layouts: 10.3 us -> 8.59 us
    dot_general x3 -> x0, matrix products: 3.61 us -> none  [dot(): return jnp.dot(left, right, preferred_element_type=F32)]
    unnamed x21 -> x14, local copies, waits for them, and re-layouts: 2.41 us -> 1.03 us
    dot_general x4 -> x3, matrix products: 2.64 us -> 1.66 us  [transpose_dot(): lax.dot_general(left, right, (((1,), (1,)), ((), ())), preferred_element_...]
    pallas_call x3 -> x2, Pallas kernels: 108 us -> 108 us  [call(): pl.pallas_call(kernel, out_shape=[jax.ShapeDtypeStruct(shape, BF16) for s...]
where the time goes in v3:
time: 122 us
  Pallas kernels  108 us (89%)
  local copies, waits for them, and re-layouts  8.59 us (7%)
  matrix products  4.08 us (3%)
    pallas_call x2, Pallas kernels, call(): pl.pallas_call(kernel, out_shape=[jax.ShapeDtypeStruct(shape, BF16) for s...  108 us
    slice x5, local copies, waits for them, and re-layouts, on_device(): return (grad_x.reshape(features.shape), rows[0], rows[1], rows[2], rows[3])  2.69 us

profile of v3, /device:TPU:1, one launch (start us, length us, event | category | flops | bytes accessed | tf_op | source)
XLA Modules:
  0.0 122.1 jit_solution(10477300609300049200)
XLA Ops:
  0.6 0.0 copy-start.5
  0.6 1.6 %reshape.64.f_ref = bf16[128,512]{1,0:T(8,128)(2,1)} reshape(bf16[8,4,4,512]{3,2,1,0:T(4,128)(2,1)} %param.7) | data formatting | bytes 262144 | tf_op jit(solution)/shard_map/reshape | solution.py:379
  2.3 0.0 copy-done.5
  2.3 0.0 copy-start.6
  2.3 0.7 reshape.65.g_ref
  3.0 0.2 copy-done.6
  3.2 0.7 reshape.66.a_ref
  3.9 72.6 %shard_map.110 = (bf16[512,512]{1,0:T(8,128)(2,1)}, bf16[512,512]{1,0:T(8,128)(2,1)}, bf16[512,128]{1,0:T(8,128)(2,1)}, bf16[3,512,128]{2,1,0:T(8,128)(2,1)}, bf...) custom-call(bf16[128,512]{1,0:T(8,128)(2,1)} %reshape.64.f_ref, bf16[128,512]{1,0:T(8,128)(2,1)} %reshape.65.g_ref, ...), custom_call_target="tpu_custom_call" | custom-call | tf_op jit(solution)/shard_map/pallas_call | solution.py:352
  76.5 0.0 copy-start
  76.5 0.0 copy-start.2
  76.5 1.5 %convolution_convert_fusion = bf16[512,128]{1,0:T(8,128)(2,1)S(1)} fusion(bf16[512,512]{1,0:T(8,128)(2,1)} %get-tuple-element.16, bf16[512,128]{1,0:T(8,128)(2,1)} %get-tuple-element.17), kind=kOutput, calls=%fused_computation.3 | convolution fusion | flops 67174400 | bytes 786432 | tf_op jit(solution)/shard_map/dot_general | solution.py:367
  78.0 0.0 copy-done
  78.0 0.0 copy-done.2
  78.0 0.3 convolution_convert_fusion.3
  78.3 0.0 copy-start.1
  78.4 0.2 copy.19
  78.6 0.7 copy-done.1
  79.3 0.3 fusion.2
  79.6 0.3 fusion.1
  79.9 0.0 copy-start.3
  79.9 0.9 copy_bitcast_fusion.t_ref
  80.8 0.1 copy-done.3
  80.9 0.3 fusion.7
  81.2 0.3 convolution_add_fusion.1
  81.5 1.1 fusion
  82.6 35.1 %shard_map.111 = (bf16[8,8,16,128]{3,2,1,0:T(8,128)(2,1)}, bf16[128,512]{1,0:T(8,128)(2,1)}) custom-call(bf16[4,8,64,128]{3,2,1,0:T(8,128)(2,1)} %copy_bitcast_fusion.t_ref, bf16[4,128,512]{2,1,0:T(8,128)(2,1)} %bitcast.58), custom_call_target="tpu_custom_call" | custom-call | tf_op jit(solution)/shard_map/pallas_call | solution.py:352
  117.7 0.0 copy-start.4
  117.7 1.6 %reshape.70 = bf16[8,4,4,512]{3,2,1,0:T(4,128)(2,1)} reshape(bf16[128,512]{1,0:T(8,128)(2,1)} %get-tuple-element.19) | data formatting | bytes 262144 | tf_op jit(solution)/shard_map/reshape | solution.py:433
  119.3 0.0 copy-done.4
  119.4 0.7 copy.24
  120.1 0.7 copy.23
  120.8 0.7 copy.22
  121.4 0.7 copy.21
  (2 shorter events, 0.1 us)
Async XLA Ops:
  0.6 1.6 %copy-start.5 = (bf16[8,4,4,512]{3,2,1,0:T(4,128)(2,1)S(1)}, bf16[8,4,4,512]{3,2,1,0:T(4,128)(2,1)}, u32[]{:S(2)}) copy-start(bf16[8,4,4,512]{3,2,1,0:T(4,128)(2,1)} %param.8) | copy-start | bytes 393220
  2.3 0.9 copy-start.6
  76.5 1.5 %copy-start = (bf16[512,512]{1,0:T(8,128)(2,1)S(1)}, bf16[512,512]{1,0:T(8,128)(2,1)}, u32[]{:S(2)}) copy-start(bf16[512,512]{1,0:T(8,128)(2,1)} %get-tuple-element.13) | copy-start | bytes 1572868
  76.5 1.5 %copy-start.2 = (bf16[512,128]{1,0:T(8,128)(2,1)S(1)}, bf16[512,128]{1,0:T(8,128)(2,1)}, u32[]{:S(2)}) copy-start(bf16[512,128]{1,0:T(8,128)(2,1)} %get-tuple-element.14) | copy-start | bytes 393220
  78.3 1.0 copy-start.1
  79.9 1.0 copy-start.3
  117.7 1.6 %copy-start.4 = (bf16[8,8,16,128]{3,2,1,0:T(8,128)(2,1)S(1)}, bf16[8,8,16,128]{3,2,1,0:T(8,128)(2,1)}, u32[]{:S(2)}) copy-start(bf16[8,8,16,128]{3,2,1,0:T(8,128)(2,1)} %get-tuple-element.20) | copy-start | bytes 786436

commit v4 on v3

--- a/solution.py
+++ b/solution.py
@@ -31,26 +31,27 @@
 
 def block_kernel(
     f_ref, g_ref, a_ref, wq_ref, wk_ref, wv_ref, wo_ref,
-    fb_ref, ab_ref, gown_ref, w3_ref, dq_ref, dkv_ref,
+    h_ref, gx_ref,
+    fb_ref, ab_ref, gown_ref, w3_ref, ft, at,
     gb_ref, wob_ref, own_ref, delta_ref,
     kv, scores, part, back, qt, gt, kt, qs, gs, prob, grad, dqt, top, total,
+    terms, partial_x, xr, s1, yr, s2, zr, u, gr,
     rsend, rrecv, wsend, wrecv, osend, orecv,
     ksend, krecv, bsend, brecv,
+    xsend, xrecv, ysend, yrecv, zsend, zrecv, usend, urecv, hsend, hrecv, gsend, grecv,
 ):
     index = {axis: lax.axis_index(axis) for axis in ("gx", "gy", "gz")}
-    gy, gz = index["gy"], index["gz"]
-    tokens, width = dq_ref.shape
+    gx, gy, gz = index["gx"], index["gy"], index["gz"]
+    tokens, width = gown_ref.shape
     local = f_ref.shape[0]
     chunk = tokens // 2
     y_bit, z_bit = lax.rem(gy, 2), lax.rem(gz, 2)
     pair_z = {"gz": gz + 1 - 2 * z_bit}
     pair_y = {"gy": gy + 1 - 2 * y_bit}
     own_columns = pl.ds(pl.multiple_of(z_bit * 256 + y_bit * 128, 128), 128)
-    greet(
-        [ring("gz", gz, d) for d in range(1, 8)]
-        + [pair_y]
-        + [ring(axis, index[axis], step) for axis, step in STEPS[:4]]
-    )
+    pair_both = {"gy": pair_y["gy"], "gz": pair_z["gz"]}
+    x = lax.div(gy, 2)
+    greet([ring(axis, index[axis], d) for axis in ("gx", "gy", "gz") for d in range(1, 8)] + [pair_both])
 
     def slot_rows(slot):
         return pl.ds(pl.multiple_of(slot * local, local), local)
@@ -144,6 +145,20 @@
         for k in (4, 5, 0, 1, 2, 3):
             outward(i, k).start()
 
+    def reduce_x(m, d):
+        target = lax.rem(x + d, 4)
+        return remote(
+            terms.at[target, pl.ds(2 * m, 2)], xr.at[d - 1, pl.ds(2 * m, 2)],
+            xsend.at[d - 1, m], xrecv.at[d - 1, m], {"gy": 2 * target + y_bit},
+        )
+
+    def begin_term(m, term):
+        split = term.reshape(8, 8, 8, width)
+        for group in range(8):
+            terms[group // 2, 2 * m + group % 2] = split[:, group].reshape(64, width).astype(BF16)
+        for d in (2, 1, 3):
+            reduce_x(m, d).start()
+
     send_own(0, 1)
     for zh in range(4):
 
@@ -159,6 +174,7 @@
     total[...] = jnp.zeros_like(total)
     dqt[...] = jnp.zeros_like(dqt)
     pass_on(2)
+    ft[...] = fb_ref[...].astype(F32).T.astype(BF16)
 
     def arrived(i, slot):
         return remote(own_ref.at[i], kv.at[slot, i], ksend.at[i, slot], krecv.at[i, slot], ring("gx", index["gx"], 1))
@@ -201,6 +217,9 @@
     for head in range(2):
         rows = products[head * (width // 2) : (head + 1) * (width // 2)]
         delta_ref[:, head * tokens : (head + 1) * tokens] = jnp.sum(rows, axis=0, keepdims=True)
+
+    at[...] = ab_ref[...].astype(F32).T.astype(BF16)
+    begin_term(3, dot(at[...], gown_ref[...]))
 
     def second_pass(turn, unused):
         last = lax.div(turn, 6)
@@ -232,7 +251,9 @@
     lax.fori_loop(0, 7, second_pass, 0)
     middle = width // 2
     turned = jnp.concatenate([dqt[:middle, :tokens], dqt[middle:, tokens:]], axis=0) * 0.125
-    dq_ref[...] = turned.T.astype(BF16)
+    dq = turned.T.astype(BF16)
+    begin_term(0, dot(ft[...], dq))
+    across = transpose_dot(dq, w3_ref[0])
     for i in range(3):
         to_y[i].wait_send()
         to_z[i].wait_send()
@@ -254,64 +275,46 @@
         whole = part[0, i].astype(F32)
         for slot in range(1, 7):
             whole = whole + back[slot, i].astype(F32)
-        dkv_ref[i] = whole.astype(BF16)
-
-
-def reduce_kernel(
-    t_ref, g_ref, h_ref, gx_ref,
-    xr, s1, yr, s2, zr, u, gr,
-    xsend, xrecv, ysend, yrecv, zsend, zrecv, usend, urecv, hsend, hrecv, gsend, grecv,
-):
-    gx, gy, gz = (lax.axis_index(axis) for axis in ("gx", "gy", "gz"))
-    y_bit, z_bit = lax.rem(gy, 2), lax.rem(gz, 2)
-    x = lax.div(gy, 2)
-    other_z, other_y = gz + 1 - 2 * z_bit, gy + 1 - 2 * y_bit
-    greet(
-        [ring("gy", gy, d) for d in range(1, 8)]
-        + [ring("gx", gx, d) for d in range(1, 8)]
-        + [ring("gz", gz, d) for d in range(1, 8)]
-        + [{"gy": other_y, "gz": other_z}]
-    )
+        pair_grad = whole.astype(BF16)
+        begin_term(1 + i, dot(ft[...], pair_grad))
+        across = across + transpose_dot(pair_grad, w3_ref[1 + i])
+    partial_x[...] = across.astype(BF16)
+
+    def join(copies):
+        for copy in copies:
+            copy.wait()
 
     def run(copies):
         for copy in copies:
             copy.start()
-        return copies
-
-    def join(copies):
-        for copy in copies:
-            copy.wait()
-
-    x_copies = []
-    for d in (2, 1, 3):
-        target = lax.rem(x + d, 4)
-        x_copies.append(
-            remote(t_ref.at[target], xr.at[d - 1], xsend.at[d - 1], xrecv.at[d - 1], {"gy": 2 * target + y_bit})
-        )
-    run(x_copies)
-    parts = (
-        (2 * (1 - y_bit) + 1 - z_bit, {"gy": other_y, "gz": other_z}),
-        (2 * (1 - y_bit) + z_bit, {"gy": other_y}),
-        (2 * y_bit + 1 - z_bit, {"gz": other_z}),
+
+    owners = (
+        (2 * (1 - y_bit) + 1 - z_bit, pair_both),
+        (2 * (1 - y_bit) + z_bit, pair_y),
+        (2 * y_bit + 1 - z_bit, pair_z),
     )
-    g_copies = run(
-        [remote(g_ref.at[part], gr.at[k], gsend.at[k], grecv.at[k], dev) for k, (part, dev) in enumerate(parts)]
-    )
-    join(x_copies)
-    total = t_ref[x].astype(F32)
+    g_copies = [
+        remote(partial_x.at[slot_rows(slot)], gr.at[k], gsend.at[k], grecv.at[k], device)
+        for k, (slot, device) in enumerate(owners)
+    ]
+    run(g_copies)
+    for m in (3, 0, 1, 2):
+        for d in (2, 1, 3):
+            reduce_x(m, d).wait()
+    whole = terms[x].astype(F32)
     for d in range(3):
-        total = total + xr[d].astype(F32)
-    s1[...] = total.astype(BF16)
+        whole = whole + xr[d].astype(F32)
+    s1[...] = whole.astype(BF16)
     y_copies = []
     for d in (4, 3, 5, 2, 6, 1, 7):
         target = lax.rem(gx + d, 8)
         y_copies.append(remote(s1.at[target], yr.at[d - 1], ysend.at[d - 1], yrecv.at[d - 1], {"gx": target}))
     run(y_copies)
     join(y_copies)
-    total = s1[gx].astype(F32)
+    whole = s1[gx].astype(F32)
     for d in range(7):
-        total = total + yr[d].astype(F32)
-    s2[...] = total.reshape(8, 8, 128)
+        whole = whole + yr[d].astype(F32)
+    s2[...] = whole.reshape(8, 8, 128)
     z_copies = []
     for d in (4, 3, 5, 2, 6, 1, 7):
         target = lax.rem(gz + d, 8)
@@ -327,10 +330,10 @@
         u_copies.append(remote(u.at[gx], u.at[gx], usend.at[d - 1], urecv.at[d - 1], ring("gx", gx, d)))
     run(u_copies)
     join(g_copies)
-    total = g_ref[2 * y_bit + z_bit].astype(F32)
+    whole = partial_x[mine].astype(F32)
     for k in range(3):
-        total = total + gr[k].astype(F32)
-    gx_ref[...] = total.astype(BF16)
+        whole = whole + gr[k].astype(F32)
+    gx_ref[...] = whole.astype(BF16)
     join(u_copies)
     h_copies = []
     for d in (4, 3, 5, 2, 6, 1, 7):
@@ -363,10 +366,6 @@
     return lax.dot_general(left, right, (((1,), (1,)), ((), ())), preferred_element_type=F32)
 
 
-def token_dot(left, right):
-    return lax.dot_general(left, right, (((0,), (0,)), ((), ())), preferred_element_type=F32)
-
-
 def dot(left, right):
     return jnp.dot(left, right, preferred_element_type=F32)
 
@@ -379,11 +378,17 @@
     feature_rows = features.reshape(local, width)
     dy_rows = grad_y.reshape(local, width)
     saved_rows = attn_out.reshape(local, width)
-    fb, ab, own_gb, w3, query_grad, pair_grads = call(
+    rows, grad_x = call(
         block_kernel,
         0,
-        [(tokens, width), (tokens, width), (tokens, quarter), (3, width, quarter), (tokens, quarter), (2, tokens, quarter)],
+        [(8, 8, 16, quarter), (local, width)],
         [
+            pltpu.VMEM((tokens, width), BF16),
+            pltpu.VMEM((tokens, width), BF16),
+            pltpu.VMEM((tokens, quarter), BF16),
+            pltpu.VMEM((3, width, quarter), BF16),
+            pltpu.VMEM((width, tokens), BF16),
+            pltpu.VMEM((width, tokens), BF16),
             pltpu.VMEM((tokens, width), BF16),
             pltpu.VMEM((quarter, width), BF16),
             pltpu.VMEM((2, tokens, quarter), BF16),
@@ -402,22 +407,8 @@
             pltpu.VMEM((quarter, 2 * tokens), F32),
             pltpu.VMEM((1, 2 * tokens), F32),
             pltpu.VMEM((1, 2 * tokens), F32),
-            dma(3, 3), dma(3, 3), dma(7, 3), dma(7, 3), dma(4), dma(2),
-            dma(2, 7), dma(2, 7), dma(7), dma(7),
-        ],
-        feature_rows, dy_rows, saved_rows, w_query, w_key, w_value, w_out,
-    )
-    grads = (query_grad, pair_grads[0], pair_grads[1])
-    partial_x = sum(transpose_dot(grads[i], w3[i]) for i in range(3))
-    partial_x = partial_x.astype(BF16).reshape(4, local, width)
-    terms = jnp.stack([token_dot(fb, part) for part in grads] + [token_dot(ab, own_gb)])
-    terms = terms.astype(BF16).reshape(4, 8, 8, 8, quarter).transpose(0, 2, 1, 3, 4)
-    terms = terms.reshape(4, 8, 64, quarter)
-    rows, grad_x = call(
-        reduce_kernel,
-        1,
-        [(8, 8, 16, quarter), (local, width)],
-        [
+            pltpu.VMEM((4, 8, 64, quarter), BF16),
+            pltpu.VMEM((tokens, width), BF16),
             pltpu.VMEM((3, 8, 64, quarter), BF16),
             pltpu.VMEM((8, 64, quarter), BF16),
             pltpu.VMEM((7, 64, quarter), BF16),
@@ -425,11 +416,13 @@
             pltpu.VMEM((8, 8, quarter), F32),
             pltpu.VMEM((8, 16, quarter), BF16),
             pltpu.VMEM((3, local, width), BF16),
-            dma(3), dma(3), dma(7), dma(7), dma(7), dma(7), dma(7), dma(7), dma(7), dma(7), dma(3), dma(3),
+            dma(3, 3), dma(3, 3), dma(7, 3), dma(7, 3), dma(4), dma(2),
+            dma(2, 7), dma(2, 7), dma(7), dma(7),
+            dma(3, 4), dma(3, 4), dma(7), dma(7), dma(7), dma(7), dma(7), dma(7), dma(7), dma(7), dma(3), dma(3),
         ],
-        terms, partial_x,
+        feature_rows, dy_rows, saved_rows, w_query, w_key, w_value, w_out,
     )
-    rows = rows.astype(F32).reshape(4, 2, 8, 2, 8, quarter).transpose(0, 2, 4, 3, 1, 5).reshape(4, 64, width)
+    rows = rows.astype(F32).reshape(4, 2, 4, 2, 2, 8, quarter).transpose(2, 0, 3, 5, 4, 1, 6).reshape(4, 64, width)
     return (grad_x.reshape(features.shape), rows[0], rows[1], rows[2], rows[3])
 
 

time: 122 us -> 107 us (0.88)
  Pallas kernels: 108 us -> 98.6 us
  matrix products: 4.08 us -> 0 us
    pallas_call x2 -> x1, Pallas kernels: 108 us -> 98.6 us  [call(): pl.pallas_call(kernel, out_shape=[jax.ShapeDtypeStruct(shape, BF16) for s...]
    dot_general x7 -> x0, matrix products: 4.08 us -> none  [the longest x4 2.42 us: token_dot(): lax.dot_general(left, right, (((0,), (0,)), ((), ())), preferred_element_...]
where the time goes in v4:
time: 107 us
  Pallas kernels  98.6 us (92%)
  local copies, waits for them, and re-layouts  7.59 us (7%)
    pallas_call x1, Pallas kernels, call(): pl.pallas_call(kernel, out_shape=[jax.ShapeDtypeStruct(shape, BF16) for s...  98.6 us
    slice x5, local copies, waits for them, and re-layouts, on_device(): return (grad_x.reshape(features.shape), rows[0], rows[1], rows[2], rows[3])  2.7 us

profile of v4, /device:TPU:1, one launch (start us, length us, event | category | flops | bytes accessed | tf_op | source)
XLA Modules:
  0.0 106.9 jit_solution(3626389200961818426)
XLA Ops:
  0.6 0.0 copy-start.1
  0.6 1.6 %reshape.35.f_ref = bf16[128,512]{1,0:T(8,128)(2,1)} reshape(bf16[8,4,4,512]{3,2,1,0:T(4,128)(2,1)} %param.7) | data formatting | bytes 262144 | tf_op jit(solution)/shard_map/reshape | solution.py:378
  2.3 0.0 copy-done.1
  2.3 0.0 copy-start.2
  2.3 0.7 reshape.36.g_ref
  3.0 0.2 copy-done.2
  3.2 0.7 reshape.37.a_ref
  3.9 98.6 %shard_map.110 = (bf16[8,8,16,128]{3,2,1,0:T(8,128)(2,1)}, bf16[128,512]{1,0:T(8,128)(2,1)}) custom-call(bf16[128,512]{1,0:T(8,128)(2,1)} %reshape.35.f_ref, bf16[128,512]{1,0:T(8,128)(2,1)} %reshape.36.g_ref, bf16[128,512]{1,0:T(8,128)(2,1)} %reshape.37.a_ref, bf16[64,512]{1,0:T(8,128)(2,1)} %wq_ref.1, bf16[64,512]{1,0:T(8,128)(2,1)} %wk_ref.1, ...), custom_call_target="tpu_custom_call" | custom-call | tf_op jit(solution)/shard_map/pallas_call | solution.py:355
  102.5 0.0 copy-start
  102.5 1.6 %reshape.38 = bf16[8,4,4,512]{3,2,1,0:T(4,128)(2,1)} reshape(bf16[128,512]{1,0:T(8,128)(2,1)} %get-tuple-element.7) | data formatting | bytes 262144 | tf_op jit(solution)/shard_map/reshape | solution.py:426
  104.1 0.0 copy-done
  104.2 0.7 copy.15
  104.9 0.7 copy.14
  105.6 0.7 copy.13
  106.2 0.7 copy.12
  (2 shorter events, 0.1 us)
Async XLA Ops:
  0.6 1.6 %copy-start.1 = (bf16[8,4,4,512]{3,2,1,0:T(4,128)(2,1)S(1)}, bf16[8,4,4,512]{3,2,1,0:T(4,128)(2,1)}, u32[]{:S(2)}) copy-start(bf16[8,4,4,512]{3,2,1,0:T(4,128)(2,1)} %param.8) | copy-start | bytes 393220
  2.3 0.9 copy-start.2
  102.5 1.6 %copy-start = (bf16[8,8,16,128]{3,2,1,0:T(8,128)(2,1)S(1)}, bf16[8,8,16,128]{3,2,1,0:T(8,128)(2,1)}, u32[]{:S(2)}) copy-start(bf16[8,8,16,128]{3,2,1,0:T(8,128)(2,1)} %get-tuple-element.8) | copy-start | bytes 786436

commit v5 on v4

--- a/solution.py
+++ b/solution.py
@@ -30,8 +30,9 @@
 
 
 def block_kernel(
-    f_ref, g_ref, a_ref, wq_ref, wk_ref, wv_ref, wo_ref,
+    f_in, g_in, a_in, wq_ref, wk_ref, wv_ref, wo_ref,
     h_ref, gx_ref,
+    f_ref, g_ref, a_ref, stage,
     fb_ref, ab_ref, gown_ref, w3_ref, ft, at,
     gb_ref, wob_ref, own_ref, delta_ref,
     kv, scores, part, back, qt, gt, kt, qs, gs, prob, grad, dqt, top, total,
@@ -58,6 +59,13 @@
 
     mine = slot_rows(2 * y_bit + z_bit)
     theirs = slot_rows(2 * (1 - y_bit) + z_bit)
+
+    def flatten(source, target):
+        for i in range(source.shape[0]):
+            for j in range(4):
+                stage[16 * i + 4 * j : 16 * i + 4 * j + 4] = source[i, j].astype(F32)
+        target[...] = stage[...].astype(BF16)
+
     trios = ((f_ref, fb_ref), (g_ref, gb_ref), (a_ref, ab_ref))
     to_y = [remote(src, dst.at[mine], rsend.at[0, i], rrecv.at[0, i], pair_y) for i, (src, dst) in enumerate(trios)]
     to_z = [remote(src, dst.at[mine], rsend.at[1, i], rrecv.at[1, i], pair_z) for i, (src, dst) in enumerate(trios)]
@@ -84,6 +92,7 @@
         return remote(wo_ref, wob_ref.at[out_rows], osend.at[zh], orecv.at[half], {"gz": 2 * zh + out_core})
 
     def begin_share(i):
+        flatten((f_in, g_in, a_in)[i], trios[i][0])
         to_y[i].start()
         to_z[i].start()
         src, dst = trios[i]
@@ -224,7 +233,7 @@
     def second_pass(turn, unused):
         last = lax.div(turn, 6)
         group = lax.div(turn, 2)
-        slot = (1 + 2 * (2 * group - 3 * lax.div(group, 2)) + lax.rem(turn, 2)) * (1 - last)
+        slot = (1 + 2 * lax.rem(group + 2, 3) + lax.rem(turn, 2)) * (1 - last)
 
         @pl.when(turn < 6)
         def _():
@@ -269,7 +278,7 @@
     for i in range(2):
         for k in range(6):
             outward(i, k).wait_send()
-    for slot in (1, 2, 5, 6, 3, 4):
+    for slot in (5, 6, 1, 2, 3, 4):
         homeward(slot).wait()
     for i in range(2):
         whole = part[0, i].astype(F32)
@@ -343,6 +352,20 @@
     join(h_copies)
 
 
+def finish_kernel(h_ref, g_ref, gx_ref, *out_refs):
+    for gy in range(8):
+        for gx in range(8):
+            x, y_bit, m, r = gy // 2, gy % 2, gx // 2, gx % 2
+            tile = h_ref[gy, gx].astype(F32)
+            for z_bit in range(2):
+                column = (2 * z_bit + y_bit) * 128
+                out_refs[m][16 * x + 8 * r : 16 * x + 8 * r + 8, column : column + 128] = tile[8 * z_bit : 8 * z_bit + 8]
+    for i in range(gx_ref.shape[0]):
+        rows = g_ref[16 * i : 16 * i + 16].astype(F32)
+        for j in range(4):
+            gx_ref[i, j] = rows[4 * j : 4 * j + 4].astype(BF16)
+
+
 def vmem(count):
     return [pl.BlockSpec(memory_space=pltpu.VMEM)] * count
 
@@ -375,14 +398,15 @@
     local = features.shape[0] * features.shape[1] * features.shape[2]
     tokens = 4 * local
     quarter = width // 4
-    feature_rows = features.reshape(local, width)
-    dy_rows = grad_y.reshape(local, width)
-    saved_rows = attn_out.reshape(local, width)
     rows, grad_x = call(
         block_kernel,
         0,
         [(8, 8, 16, quarter), (local, width)],
         [
+            pltpu.VMEM((local, width), BF16),
+            pltpu.VMEM((local, width), BF16),
+            pltpu.VMEM((local, width), BF16),
+            pltpu.VMEM((local, width), F32),
             pltpu.VMEM((tokens, width), BF16),
             pltpu.VMEM((tokens, width), BF16),
             pltpu.VMEM((tokens, quarter), BF16),
@@ -420,10 +444,15 @@
             dma(2, 7), dma(2, 7), dma(7), dma(7),
             dma(3, 4), dma(3, 4), dma(7), dma(7), dma(7), dma(7), dma(7), dma(7), dma(7), dma(7), dma(3), dma(3),
         ],
-        feature_rows, dy_rows, saved_rows, w_query, w_key, w_value, w_out,
+        features, grad_y, attn_out, w_query, w_key, w_value, w_out,
     )
-    rows = rows.astype(F32).reshape(4, 2, 4, 2, 2, 8, quarter).transpose(2, 0, 3, 5, 4, 1, 6).reshape(4, 64, width)
-    return (grad_x.reshape(features.shape), rows[0], rows[1], rows[2], rows[3])
+    outs = pl.pallas_call(
+        finish_kernel,
+        out_shape=[jax.ShapeDtypeStruct(features.shape, BF16)] + [jax.ShapeDtypeStruct((64, width), F32)] * 4,
+        in_specs=vmem(2),
+        out_specs=vmem(5),
+    )(rows, grad_x)
+    return tuple(outs)
 
 
 def solution(mesh):

time: 107 us -> 100 us (0.935)
  local copies, waits for them, and re-layouts: 7.59 us -> 0 us
    reshape x4 -> x0, local copies, waits for them, and re-layouts: 4.65 us -> none  [the longest x1 1.64 us: on_device(): return (grad_x.reshape(features.shape), rows[0], rows[1], rows[2], rows[3])]
    slice x5 -> x0, local copies, waits for them, and re-layouts: 2.7 us -> none  [on_device(): return (grad_x.reshape(features.shape), rows[0], rows[1], rows[2], rows[3])]
    pallas_call x0 -> x1, Pallas kernels: none -> 1.83 us  [on_device(): pl.pallas_call(finish_kernel, out_shape=[jax.ShapeDtypeStruct(features.sh...]
    pallas_call x1, Pallas kernels: 98.6 us -> 97.4 us  [call(): pl.pallas_call(kernel, out_shape=[jax.ShapeDtypeStruct(shape, BF16) for s...]
where the time goes in v5:
time: 100 us; the launch traced here: 99.9 us
  Pallas kernels  99.2 us (99%)
    pallas_call x1, Pallas kernels, call(): pl.pallas_call(kernel, out_shape=[jax.ShapeDtypeStruct(shape, BF16) for s...  97.4 us

profile of v5, /device:TPU:1, one launch (start us, length us, event | category | flops | bytes accessed | tf_op | source)
XLA Modules:
  0.0 99.9 jit_solution(17158990784383490392)
XLA Ops:
  0.6 97.4 %shard_map.110 = (bf16[8,8,16,128]{3,2,1,0:T(8,128)(2,1)}, bf16[128,512]{1,0:T(8,128)(2,1)}) custom-call(bf16[8,4,4,512]{3,2,1,0:T(4,128)(2,1)} %f_in.1, bf16[8,4,4,512]{3,2,1,0:T(4,128)(2,1)} %g_in.1, bf16[8,4,4,512]{3,2,1,0:T(4,128)(2,1)} %a_in.1, bf16[64,512]{1,0:T(8,128)(2,1)} %wq_ref.1, bf16[64,512]{1,0:T(8,128)(2,1)} %wk_ref.1, ...), custom_call_target="tpu_custom_call" | custom-call | tf_op jit(solution)/shard_map/pallas_call | solution.py:378
  98.1 1.8 %shard_map.111 = (bf16[8,4,4,512]{3,2,1,0:T(4,128)(2,1)}, f32[64,512]{1,0:T(8,128)}, f32[64,512]{1,0:T(8,128)}, f32[64,512]{1,0:T(8,128)}, f32[64,512]{1,0:T(8,128)}) custom-call(bf16[8,8,16,128]{3,2,1,0:T(8,128)(2,1)} %get-tuple-element.7.h_ref, bf16[128,512]{1,0:T(8,128)(2,1)} %get-tuple-element.8.g_ref), custom_call_target="tpu_custom_call" | custom-call | tf_op jit(solution)/shard_map/pallas_call | solution.py:449

commit v6 on v5

--- a/solution.py
+++ b/solution.py
@@ -37,7 +37,7 @@
     gb_ref, wob_ref, own_ref, delta_ref,
     kv, scores, part, back, qt, gt, kt, qs, gs, prob, grad, dqt, top, total,
     terms, partial_x, xr, s1, yr, s2, zr, u, gr,
-    rsend, rrecv, wsend, wrecv, osend, orecv,
+    rsend, rrecv, wsend, wrecv, osend, orecv, vsend, vrecv,
     ksend, krecv, bsend, brecv,
     xsend, xrecv, ysend, yrecv, zsend, zrecv, usend, urecv, hsend, hrecv, gsend, grecv,
 ):
@@ -74,22 +74,30 @@
         for i, (src, dst) in enumerate(trios)
     ]
     weights = (wq_ref, wk_ref, wv_ref)
-    weight_rows = pl.ds(pl.multiple_of(gz * 64, 64), 64)
+    x_rows = pl.ds(pl.multiple_of(x * 16, 16), 16)
+
+    def x_peer(d):
+        return {"gy": 2 * lax.rem(x + d, 4) + y_bit}
+
+    def weight_share(i, d):
+        return remote(w3_ref.at[i, :, x], w3_ref.at[i, :, x], vsend.at[d - 1, i], vrecv.at[d - 1, i], x_peer(d))
+
+    def out_share(d):
+        return remote(wob_ref.at[:, x], wob_ref.at[:, x], vsend.at[d - 1, 3], vrecv.at[d - 1, 3], x_peer(d))
 
     def weight_copy(i, d):
         target = lax.rem(gz + d, 8)
         columns = pl.ds(pl.multiple_of(lax.rem(target, 2) * 256 + y_bit * 128, 128), 128)
         return remote(
-            weights[i].at[:, columns], w3_ref.at[i, weight_rows], wsend.at[d - 1, i], wrecv.at[d - 1, i], {"gz": target}
+            weights[i].at[x_rows, columns], w3_ref.at[i, gz, x], wsend.at[d - 1, i], wrecv.at[d - 1, i], {"gz": target}
         )
 
     half = lax.rem(gz, 2)
     out_core = lax.div(gz, 4)
     out_from = lax.rem(lax.div(gz, 2), 2) == y_bit
-    out_rows = pl.ds(pl.multiple_of(half * 64, 64), 64)
 
     def out_copy(zh):
-        return remote(wo_ref, wob_ref.at[out_rows], osend.at[zh], orecv.at[half], {"gz": 2 * zh + out_core})
+        return remote(wo_ref.at[x_rows], wob_ref.at[half, x], osend.at[zh], orecv.at[half], {"gz": 2 * zh + out_core})
 
     def begin_share(i):
         flatten((f_in, g_in, a_in)[i], trios[i][0])
@@ -111,15 +119,39 @@
     for i in (1, 0, 2):
         for d in order:
             weight_copy(i, d).start()
-        w3_ref[i, weight_rows] = weights[i][:, own_columns]
+        w3_ref[i, gz, x] = weights[i][x_rows, own_columns]
+    for zh in range(4):
+
+        @pl.when(jnp.logical_and(out_from, 2 * zh + out_core != gz))
+        def _():
+            out_copy(zh).start()
+
     begin_share(1)
     pass_on(0)
-    end_share(0)
-
-    def project(i):
+    for i in (1, 0, 2):
         for d in order:
             weight_copy(i, d).wait_recv()
-        return dot(fb_ref[...], w3_ref[i])
+        for d in (2, 1, 3):
+            weight_share(i, d).start()
+    for s in range(2):
+        source = 4 * z_bit + 2 * y_bit + s
+
+        @pl.when(source != gz)
+        def _():
+            remote(wo_ref.at[x_rows], wob_ref.at[s, x], osend.at[0], orecv.at[s], {"gz": source}).wait_recv()
+
+        @pl.when(source == gz)
+        def _():
+            wob_ref[s, x] = wo_ref[x_rows]
+
+    for d in (2, 1, 3):
+        out_share(d).start()
+    end_share(0)
+
+    def project(i):
+        for d in (2, 1, 3):
+            weight_share(i, d).wait_recv()
+        return dot(fb_ref[...], w3_ref[i].reshape(tokens, width))
 
     def outward(i, k):
         axis, step = STEPS[k]
@@ -169,12 +201,6 @@
             reduce_x(m, d).start()
 
     send_own(0, 1)
-    for zh in range(4):
-
-        @pl.when(jnp.logical_and(out_from, 2 * zh + out_core != gz))
-        def _():
-            out_copy(zh).start()
-
     begin_share(2)
     send_own(1, 2)
     pass_on(1)
@@ -206,21 +232,12 @@
 
     lax.fori_loop(0, 7, first_pass, 0)
     top[...] = top[...] + jnp.log(total[...])
-    for s in range(2):
-        source = 4 * z_bit + 2 * y_bit + s
-
-        @pl.when(source != gz)
-        def _():
-            remote(wo_ref, wob_ref.at[pl.ds(s * 64, 64)], osend.at[0], orecv.at[s], {"gz": source}).wait_recv()
-
-        @pl.when(source == gz)
-        def _():
-            wob_ref[pl.ds(s * 64, 64)] = wo_ref[...]
-
+    for d in (2, 1, 3):
+        out_share(d).wait_recv()
     end_share(1)
     end_share(2)
     gown_ref[...] = gb_ref[:, own_columns]
-    upstream = transpose_dot(gb_ref[...], wob_ref[...]).astype(BF16).astype(F32)
+    upstream = transpose_dot(gb_ref[...], wob_ref[...].reshape(width, gb_ref.shape[1])).astype(BF16).astype(F32)
     spread(upstream, gt, gs)
     products = (upstream * ab_ref[:, own_columns].astype(F32)).T
     for head in range(2):
@@ -262,13 +279,17 @@
     turned = jnp.concatenate([dqt[:middle, :tokens], dqt[middle:, tokens:]], axis=0) * 0.125
     dq = turned.T.astype(BF16)
     begin_term(0, dot(ft[...], dq))
-    across = transpose_dot(dq, w3_ref[0])
+    across = transpose_dot(dq, w3_ref[0].reshape(tokens, width))
     for i in range(3):
         to_y[i].wait_send()
         to_z[i].wait_send()
         onward[i].wait_send()
         for d in order:
             weight_copy(i, d).wait_send()
+        for d in (2, 1, 3):
+            weight_share(i, d).wait_send()
+    for d in (2, 1, 3):
+        out_share(d).wait_send()
     for zh in range(4):
 
         @pl.when(jnp.logical_and(out_from, 2 * zh + out_core != gz))
@@ -286,7 +307,7 @@
             whole = whole + back[slot, i].astype(F32)
         pair_grad = whole.astype(BF16)
         begin_term(1 + i, dot(ft[...], pair_grad))
-        across = across + transpose_dot(pair_grad, w3_ref[1 + i])
+        across = across + transpose_dot(pair_grad, w3_ref[1 + i].reshape(tokens, width))
     partial_x[...] = across.astype(BF16)
 
     def join(copies):
@@ -410,11 +431,11 @@
             pltpu.VMEM((tokens, width), BF16),
             pltpu.VMEM((tokens, width), BF16),
             pltpu.VMEM((tokens, quarter), BF16),
-            pltpu.VMEM((3, width, quarter), BF16),
+            pltpu.VMEM((3, 8, 4, 16, quarter), BF16),
             pltpu.VMEM((width, tokens), BF16),
             pltpu.VMEM((width, tokens), BF16),
             pltpu.VMEM((tokens, width), BF16),
-            pltpu.VMEM((quarter, width), BF16),
+            pltpu.VMEM((2, 4, 16, width), BF16),
             pltpu.VMEM((2, tokens, quarter), BF16),
             pltpu.VMEM((1, 2 * tokens), F32),
             pltpu.VMEM((7, 2, tokens, quarter), BF16),
@@ -440,7 +461,7 @@
             pltpu.VMEM((8, 8, quarter), F32),
             pltpu.VMEM((8, 16, quarter), BF16),
             pltpu.VMEM((3, local, width), BF16),
-            dma(3, 3), dma(3, 3), dma(7, 3), dma(7, 3), dma(4), dma(2),
+            dma(3, 3), dma(3, 3), dma(7, 3), dma(7, 3), dma(4), dma(2), dma(3, 4), dma(3, 4),
             dma(2, 7), dma(2, 7), dma(7), dma(7),
             dma(3, 4), dma(3, 4), dma(7), dma(7), dma(7), dma(7), dma(7), dma(7), dma(7), dma(7), dma(3), dma(3),
         ],

time: 100 us -> 93.7 us (0.937)
  Pallas kernels: 99.2 us -> 92.9 us
    pallas_call x1, Pallas kernels: 97.4 us -> 91.1 us  [call(): pl.pallas_call(kernel, out_shape=[jax.ShapeDtypeStruct(shape, BF16) for s...]
where the time goes in v6:
time: 93.7 us; the launch traced here: 93.5 us
  Pallas kernels  92.9 us (99%)
    pallas_call x1, Pallas kernels, call(): pl.pallas_call(kernel, out_shape=[jax.ShapeDtypeStruct(shape, BF16) for s...  91.1 us

profile of v6, /device:TPU:1, one launch (start us, length us, event | category | flops | bytes accessed | tf_op | source)
XLA Modules:
  0.0 93.5 jit_solution(17904105260884618723)
XLA Ops:
  0.6 91.1 %shard_map.110 = (bf16[8,8,16,128]{3,2,1,0:T(8,128)(2,1)}, bf16[128,512]{1,0:T(8,128)(2,1)}) custom-call(bf16[8,4,4,512]{3,2,1,0:T(4,128)(2,1)} %f_in.1, bf16[8,4,4,512]{3,2,1,0:T(4,128)(2,1)} %g_in.1, bf16[8,4,4,512]{3,2,1,0:T(4,128)(2,1)} %a_in.1, bf16[64,512]{1,0:T(8,128)(2,1)} %wq_ref.1, bf16[64,512]{1,0:T(8,128)(2,1)} %wk_ref.1, ...), custom_call_target="tpu_custom_call" | custom-call | tf_op jit(solution)/shard_map/pallas_call | solution.py:399
  91.7 1.8 %shard_map.111 = (bf16[8,4,4,512]{3,2,1,0:T(4,128)(2,1)}, f32[64,512]{1,0:T(8,128)}, f32[64,512]{1,0:T(8,128)}, f32[64,512]{1,0:T(8,128)}, f32[64,512]{1,0:T(8,128)}) custom-call(bf16[8,8,16,128]{3,2,1,0:T(8,128)(2,1)} %get-tuple-element.7.h_ref, bf16[128,512]{1,0:T(8,128)(2,1)} %get-tuple-element.8.g_ref), custom_call_target="tpu_custom_call" | custom-call | tf_op jit(solution)/shard_map/pallas_call | solution.py:470

commit v7 on v6

--- a/solution.py
+++ b/solution.py
@@ -18,10 +18,11 @@
     )
 
 
-def greet(devices):
+def greet(devices, meanwhile):
     barrier = pltpu.get_barrier_semaphore()
     for device in devices:
         pl.semaphore_signal(barrier, inc=1, device_id=device, device_id_type=MESH)
+    meanwhile()
     pl.semaphore_wait(barrier, len(devices))
 
 
@@ -52,19 +53,19 @@
     own_columns = pl.ds(pl.multiple_of(z_bit * 256 + y_bit * 128, 128), 128)
     pair_both = {"gy": pair_y["gy"], "gz": pair_z["gz"]}
     x = lax.div(gy, 2)
-    greet([ring(axis, index[axis], d) for axis in ("gx", "gy", "gz") for d in range(1, 8)] + [pair_both])
-
-    def slot_rows(slot):
-        return pl.ds(pl.multiple_of(slot * local, local), local)
-
-    mine = slot_rows(2 * y_bit + z_bit)
-    theirs = slot_rows(2 * (1 - y_bit) + z_bit)
-
     def flatten(source, target):
         for i in range(source.shape[0]):
             for j in range(4):
                 stage[16 * i + 4 * j : 16 * i + 4 * j + 4] = source[i, j].astype(F32)
         target[...] = stage[...].astype(BF16)
+
+    greet([ring(axis, index[axis], d) for axis in ("gx", "gy", "gz") for d in range(1, 8)] + [pair_both], lambda: flatten(f_in, f_ref))
+
+    def slot_rows(slot):
+        return pl.ds(pl.multiple_of(slot * local, local), local)
+
+    mine = slot_rows(2 * y_bit + z_bit)
+    theirs = slot_rows(2 * (1 - y_bit) + z_bit)
 
     trios = ((f_ref, fb_ref), (g_ref, gb_ref), (a_ref, ab_ref))
     to_y = [remote(src, dst.at[mine], rsend.at[0, i], rrecv.at[0, i], pair_y) for i, (src, dst) in enumerate(trios)]
@@ -100,7 +101,8 @@
         return remote(wo_ref.at[x_rows], wob_ref.at[half, x], osend.at[zh], orecv.at[half], {"gz": 2 * zh + out_core})
 
     def begin_share(i):
-        flatten((f_in, g_in, a_in)[i], trios[i][0])
+        if i > 0:
+            flatten((f_in, g_in, a_in)[i], trios[i][0])
         to_y[i].start()
         to_z[i].start()
         src, dst = trios[i]

time: 93.7 us -> 93.6 us (level)
  no operation moved by 1% of the time
where the time goes in v7:
time: 93.6 us; the launch traced here: 93.1 us
  Pallas kernels  92.5 us (99%)
    pallas_call x1, Pallas kernels, call(): pl.pallas_call(kernel, out_shape=[jax.ShapeDtypeStruct(shape, BF16) for s...  90.6 us

profile of v7, /device:TPU:1, one launch (start us, length us, event | category | flops | bytes accessed | tf_op | source)
XLA Modules:
  0.0 93.1 jit_solution(6654671459195303887)
XLA Ops:
  0.6 90.6 %shard_map.110 = (bf16[8,8,16,128]{3,2,1,0:T(8,128)(2,1)}, bf16[128,512]{1,0:T(8,128)(2,1)}) custom-call(bf16[8,4,4,512]{3,2,1,0:T(4,128)(2,1)} %f_in.1, bf16[8,4,4,512]{3,2,1,0:T(4,128)(2,1)} %g_in.1, bf16[8,4,4,512]{3,2,1,0:T(4,128)(2,1)} %a_in.1, bf16[64,512]{1,0:T(8,128)(2,1)} %wq_ref.1, bf16[64,512]{1,0:T(8,128)(2,1)} %wk_ref.1, ...), custom_call_target="tpu_custom_call" | custom-call | tf_op jit(solution)/shard_map/pallas_call | solution.py:401
  91.3 1.8 %shard_map.111 = (bf16[8,4,4,512]{3,2,1,0:T(4,128)(2,1)}, f32[64,512]{1,0:T(8,128)}, f32[64,512]{1,0:T(8,128)}, f32[64,512]{1,0:T(8,128)}, f32[64,512]{1,0:T(8,128)}) custom-call(bf16[8,8,16,128]{3,2,1,0:T(8,128)(2,1)} %get-tuple-element.7.h_ref, bf16[128,512]{1,0:T(8,128)(2,1)} %get-tuple-element.8.g_ref), custom_call_target="tpu_custom_call" | custom-call | tf_op jit(solution)/shard_map/pallas_call | solution.py:472
